TPU v7x, 128 devices: a whole 4x4x4 slice. The times are simulated.
128 devices in a mesh: row: 8 (over x, z_lo), col: 16 (over z_hi, y, core).
Axes of the slice: x: 4, y: 4, z: 4 (z_hi: 2, z_lo: 2; z = z_hi * 2 + z_lo), core: 2. Of those that a mesh axis runs over, the one named last changes fastest.
Arguments:
- image: bfloat16 [128, 512, 768], P('row', 'col'), may hold values from -6 to 6
- conv_taps: float32 [9, 768], replicated, may hold values from -0.5 to 0.5
- w_query: bfloat16 [768, 768], replicated, may hold values from -0.21875 to 0.21875
- w_key: bfloat16 [768, 768], replicated, may hold values from -0.21875 to 0.21875
- w_value: bfloat16 [768, 768], replicated, may hold values from -0.21875 to 0.21875
- w_out: bfloat16 [768, 768], replicated, may hold values from -0.21875 to 0.21875
- grad_out: bfloat16 [128, 512, 768], P('row', 'col'), may hold values from -6 to 6
Outputs:
- grad_image: bfloat16 [128, 512, 768], P('row', 'col')
- grad_weights: float32 [768, 3072], P(None, 'col')
- grad_conv: float32 [9, 768], P(None, 'col')
All inputs are finite; a program needn't handle non-finite values.
Results may differ from a plain program's by a relative error of at most 0.022.
Values may be sent and summed in bfloat16 or wider, within the bound.
No kernel may reach another device: no remote copies, remote signals or barrier semaphores. Data moves between devices by JAX's collectives and lax.ppermute only.
A program may use at most 128 MiB of HBM per device.

v0:
```python
from functools import partial
import math

import jax
import jax.numpy as jnp
from jax import lax
from jax.sharding import PartitionSpec as P

HEADS = 12
HD = 64
POOL = 8


EPSILON = 1e-05


def with_halo(cells, sides, width):
    for axis, dim in sides:
        count = lax.axis_size(axis)
        ends = count - 1
        head = lax.slice_in_dim(cells, 0, width, axis=dim)
        tail = lax.slice_in_dim(cells, cells.shape[dim] - width, cells.shape[dim], axis=dim)
        cells = jnp.concatenate(
            [
                lax.ppermute(tail, axis, [(i, (i + 1) % count) for i in range(ends)]),
                cells,
                lax.ppermute(head, axis, [((i + 1) % count, i) for i in range(ends)]),
            ],
            axis=dim,
        )
    return cells


def copy_for_each(x, axis):
    peers = lax.axis_size(axis)
    return lax.all_to_all(jnp.broadcast_to(x[None], (peers, *x.shape)), axis, 0, 0, tiled=True)


def in_order(parts, dim):
    parts = jnp.moveaxis(parts, 0, dim)
    lengths = parts.shape
    return parts.reshape(*lengths[:dim], lengths[dim] * lengths[dim + 1], *lengths[dim + 2 :])


def gather_directly(x, axis, dim):
    parts = copy_for_each(x, axis)
    return in_order(parts, dim)


def cut_along(x, dim, peers):
    lengths = x.shape
    parts = x.reshape(*lengths[:dim], peers, lengths[dim] // peers, *lengths[dim + 1 :])
    return jnp.moveaxis(parts, dim, 0)


def sum_at_owner(x, axis, dim):
    peers = lax.axis_size(axis)
    parts = lax.all_to_all(cut_along(x, dim, peers), axis, 0, 0, tiled=True)
    return jnp.sum(parts.astype(jnp.float32), axis=0)


def sum_together(arrays, axis, dims):
    peers = lax.axis_size(axis)
    parts = [cut_along(a, dim, peers) for a, dim in zip(arrays, dims)]
    lines = jnp.concatenate([b.reshape(peers, -1) for b in parts], axis=1)
    rows = max(16, -(-lines.shape[1] // 1024) * 8)
    lines = jnp.pad(lines, ((0, 0), (0, rows * 128 - lines.shape[1]))).reshape(-1, 128)
    ravelled, at, gathered = (lax.psum_scatter(lines, axis, tiled=True).reshape(-1), 0, [])
    for b in parts:
        part = b[0]
        gathered.append(ravelled[at : at + part.size].reshape(part.shape))
        at += part.size
    return tuple(gathered)


def taken_together(x, axis):
    return copy_for_each(x, axis).astype(jnp.float32).sum(axis=0)


def contract_first(left, right):
    return lax.dot_general(
        left, right, (((0,), (0,)), ((), ())), preferred_element_type=jnp.float32
    )


def contract_last(left, right):
    return lax.dot_general(
        left, right, (((1,), (1,)), ((), ())), preferred_element_type=jnp.float32
    )


def exact_first(left, right):
    return lax.dot_general(
        left,
        right,
        (((0,), (0,)), ((), ())),
        precision=lax.Precision.HIGHEST,
        preferred_element_type=jnp.float32,
    )


def exact_last(left, right):
    return lax.dot_general(
        left,
        right,
        (((1,), (1,)), ((), ())),
        precision=lax.Precision.HIGHEST,
        preferred_element_type=jnp.float32,
    )


def stencil(padded, taps, height, width, flipped):
    total = jnp.zeros((height, width, padded.shape[2]), jnp.float32)
    for tap_row in range(3):
        for tap_col in range(3):
            if flipped:
                window = padded[
                    2 - tap_row : 2 - tap_row + height, 2 - tap_col : 2 - tap_col + width
                ]
            else:
                window = padded[tap_row : tap_row + height, tap_col : tap_col + width]
            total = total + taps[3 * tap_row + tap_col] * window.astype(jnp.float32)
    return total


def attend(carry, inputs, key_heads, value_heads):
    grad_key, grad_value = carry
    query_block, dout_block = inputs
    softmax_scale = HD ** (-0.5)
    query_heads = query_block.reshape(-1, HEADS, HD)
    dout_heads = dout_block.reshape(-1, HEADS, HD)
    scores = (
        jnp.einsum("qhd,khd->hqk", query_heads, key_heads, preferred_element_type=jnp.float32)
        * softmax_scale
    )
    expons = jnp.exp(scores)
    probabilities = expons / jnp.sum(expons, axis=-1, keepdims=True)
    weights = probabilities.astype(jnp.bfloat16)
    attended = jnp.einsum(
        "hqk,khd->qhd", weights, value_heads, preferred_element_type=jnp.float32
    ).astype(jnp.bfloat16)
    grad_probs = jnp.einsum(
        "qhd,khd->hqk", dout_heads, value_heads, preferred_element_type=jnp.float32
    )
    deltas = jnp.einsum("qhd,qhd->hq", dout_heads, attended, preferred_element_type=jnp.float32)
    grad_scores = (probabilities * (grad_probs - deltas[:, :, None]) * softmax_scale).astype(
        jnp.bfloat16
    )
    grad_query = jnp.einsum(
        "hqk,khd->qhd", grad_scores, key_heads, preferred_element_type=jnp.float32
    ).astype(jnp.bfloat16)
    grad_key = grad_key + jnp.einsum(
        "hqk,qhd->khd", grad_scores, query_heads, preferred_element_type=jnp.float32
    )
    grad_value = grad_value + jnp.einsum(
        "hqk,qhd->khd", weights, dout_heads, preferred_element_type=jnp.float32
    )
    return (
        (grad_key, grad_value),
        (attended.reshape(query_block.shape), grad_query.reshape(query_block.shape)),
    )


def on_device(image, conv_taps, w_query, w_key, w_value, w_out, grad_out):
    height, width, channels = image.shape
    padded = with_halo(image, (("row", 0), ("col", 1)), 1)
    mixed = image.astype(jnp.float32) + stencil(padded, conv_taps, height, width, False)
    hidden = mixed.astype(jnp.bfloat16)
    flat_hidden = hidden.reshape(-1, channels)
    query = jnp.dot(flat_hidden, w_query, preferred_element_type=jnp.float32).astype(jnp.bfloat16)
    pooled = (
        hidden.astype(jnp.float32)
        .reshape(height // POOL, POOL, width // POOL, POOL, channels)
        .mean(axis=(1, 3))
    )
    centre = jnp.mean(pooled, axis=-1, keepdims=True)
    spread = jnp.mean(jnp.square(pooled - centre), axis=-1, keepdims=True)
    inverse = lax.rsqrt(spread + EPSILON)
    standard = (pooled - centre) * inverse
    normed = standard.astype(jnp.bfloat16)
    gathered = gather_directly(normed, "col", 1)
    pooled_rows, pooled_cols = (gathered.shape[0], gathered.shape[1])
    key_cells = gathered.reshape(-1, channels)
    keys = jnp.dot(key_cells, w_key, preferred_element_type=jnp.float32).astype(jnp.bfloat16)
    values = jnp.dot(key_cells, w_value, preferred_element_type=jnp.float32).astype(jnp.bfloat16)
    flat_grad = grad_out.reshape(-1, channels)
    dout = contract_last(flat_grad, w_out).astype(jnp.bfloat16)
    total_rows = flat_hidden.shape[0]
    block_rows = math.gcd(total_rows, 512)
    blocks = total_rows // block_rows
    key_heads = keys.reshape(-1, HEADS, HD)
    value_heads = values.reshape(-1, HEADS, HD)
    empty_grad = jnp.zeros(key_heads.shape, jnp.float32)
    carry, produced = lax.scan(
        partial(attend, key_heads=key_heads, value_heads=value_heads),
        (empty_grad, empty_grad),
        (query.reshape(blocks, block_rows, channels), dout.reshape(blocks, block_rows, channels)),
    )
    grad_key = carry[0].reshape(pooled_rows, pooled_cols, channels)
    grad_value = carry[1].reshape(pooled_rows, pooled_cols, channels)
    attended = produced[0].reshape(-1, channels)
    grad_query = produced[1].reshape(-1, channels)
    grad_wout = contract_first(attended, flat_grad)
    grad_wquery = contract_first(flat_hidden, grad_query)
    grad_hidden = contract_last(grad_query, w_query)
    key_float = w_key.astype(jnp.float32)
    value_float = w_value.astype(jnp.float32)
    flat_key = grad_key.reshape(-1, channels)
    flat_value = grad_value.reshape(-1, channels)
    cell_terms = exact_last(flat_key, key_float) + exact_last(flat_value, value_float)
    cells_float = key_cells.astype(jnp.float32)
    grad_wkey = exact_first(cells_float, flat_key)
    grad_wvalue = exact_first(cells_float, flat_value)
    grad_normed = sum_at_owner(
        cell_terms.reshape(pooled_rows, pooled_cols, channels).astype(jnp.bfloat16), "col", 1
    )
    grad_pooled = (
        grad_normed
        - jnp.mean(grad_normed, axis=-1, keepdims=True)
        - standard * jnp.mean(grad_normed * standard, axis=-1, keepdims=True)
    ) * inverse
    spread_back = jnp.broadcast_to(
        (grad_pooled / (POOL * POOL))[:, None, :, None, :],
        (height // POOL, POOL, width // POOL, POOL, channels),
    ).reshape(height, width, channels)
    grad_mixed = (
        grad_out.astype(jnp.float32) + grad_hidden.reshape(height, width, channels) + spread_back
    )
    grad_padded = with_halo(grad_mixed.astype(jnp.bfloat16), (("row", 0), ("col", 1)), 1).astype(
        grad_mixed.dtype
    )
    grad_image = (grad_mixed + stencil(grad_padded, conv_taps, height, width, True)).astype(
        jnp.bfloat16
    )
    tap_list = []
    for tap_row in range(3):
        for tap_col in range(3):
            window = padded[tap_row : tap_row + height, tap_col : tap_col + width].astype(
                jnp.float32
            )
            tap_list.append(jnp.sum(grad_mixed * window, axis=(0, 1)))
    tap_terms = jnp.stack(tap_list, axis=0)
    weight_terms = jnp.concatenate([grad_wquery, grad_wkey, grad_wvalue, grad_wout], axis=1)
    column_sums = tuple(
        (
            part.astype(jnp.float32)
            for part in sum_together(
                (weight_terms.astype(jnp.bfloat16), tap_terms.astype(jnp.bfloat16)), "col", (1, 1)
            )
        )
    )
    grad_weights, grad_conv = (
        taken_together(column_sums[0].astype(jnp.bfloat16), "row").astype(jnp.float32),
        taken_together(column_sums[1].astype(jnp.bfloat16), "row").astype(jnp.float32),
    )
    return (grad_image, grad_weights, grad_conv)


def solution(mesh):
    return jax.shard_map(
        on_device,
        mesh=mesh,
        in_specs=(P("row", "col", None), P(), P(), P(), P(), P(), P("row", "col", None)),
        out_specs=(P("row", "col", None), P(None, "col"), P(None, "col")),
        check_vma=False,
    )
```

profile of v0, /device:TPU:96, one launch (start us, length us, event | category | flops | bytes accessed | tf_op | source)
XLA Modules:
  0.0 357.3 jit_solution(7163266316754872919)
XLA Ops:
  8.1 3.2 collective-permute-start
  11.3 2.6 collective-permute-start.1
  14.0 3.3 convolution_convert_fusion.4
  19.1 2.8 collective-permute-start.3
  21.9 1.9 collective-permute-start.2
  27.1 4.2 %collective-permute-done.2 = bf16[18,1,768]{2,1,0:T(2,128)(2,1)} collective-permute-done((bf16[18,1,768]{2,1,0:T(2,128)(2,1)}, bf16[18,1,768]{2,1,0:T(2,128)(2,1)}, u32[]{:S(2)}, u32[]{:S(2)}) %collective-permute-start.2) | collective-permute-done | bytes 27680 | tf_op jit(solution)/shard_map/ppermute | solution.py:25
  31.3 5.2 %fusion.33 = bf16[16,32,768]{2,1,0:T(8,128)(2,1)S(1)} fusion(bf16[16,32,768]{2,1,0:T(8,128)(2,1)S(1)} %copy-done.4, bf16[1,32,768]{2,1,0:T(8,128)(2,1)} %copy-done.27, bf16[1,32,768]{2,1,0:T(8,128)(2,1)} %copy-done.25, f32[768]{0:T(1024)} %get-tuple-element.54, f32[768]{0:T(1024)} %get-tuple-element.55, f32[768]{0:T(1024)S(1)} %get-tuple-element.48, ...), kind=kLoop, calls=%fused_computation.69 | loop fusion | flops 20447232 | bytes 2638848 | tf_op jit(solution)/shard_map/convert_element_type | solution.py:168
  37.8 4.8 %all-to-all-start = ((bf16[16,2,4,768]{3,2,1,0:T(4,128)(2,1)}), bf16[16,2,4,768]{3,2,1,0:T(4,128)(2,1)}, u32[]{:S(2)}, u32[]{:S(2)}) async-start(bf16[16,2,4,768]{3,2,1,0:T(4,128)(2,1)} %broadcast_in_dim.21), calls=%async_computation | async-start | bytes 393216 | tf_op jit(solution)/shard_map/all_to_all | solution.py:36
  42.6 1.7 convolution_convert_fusion.5
  45.7 2.7 all-to-all-done
  60.7 1.8 reshape.192
  62.4 2.4 fusion.46
  67.1 6.5 %all-to-all-start.1 = ((bf16[16,2,4,768]{3,2,1,0:T(4,128)(2,1)}), bf16[16,2,4,768]{3,2,1,0:T(4,128)(2,1)S(1)}, u32[]{:S(2)}, u32[]{:S(2)}) async-start(bf16[16,2,4,768]{3,2,1,0:T(4,128)(2,1)} %bitcast.94), calls=%async_computation.1 | async-start | bytes 393216 | tf_op jit(solution)/shard_map/all_to_all | solution.py:58
  78.0 2.5 maximum_bitcast_fusion
  80.5 2.9 copy.100
  83.4 2.0 dot_general.88
  85.5 7.9 %copy.106 = bf16[16,768,192]{2,1,0:T(8,128)(2,1)} copy(bf16[16,768,192]{1,2,0:T(8,128)(2,1)} %maximum_bitcast_fusion) | data formatting | bytes 9437184 | tf_op jit(solution)/shard_map/transpose | solution.py:53
  93.4 10.9 %reshape.181 = bf16[16,147456]{1,0:T(8,128)(2,1)} reshape(bf16[16,768,192]{2,1,0:T(8,128)(2,1)} %copy.106) | data formatting | bytes 9437184 | tf_op jit(solution)/shard_map/reshape | solution.py:65
  105.7 6.1 %fusion.20 = (bf16[768]{0:T(1024)(128)(2,1)S(1)}, bf16[768]{0:T(1024)(128)(2,1)S(1)}, bf16[768]{0:T(1024)(128)(2,1)S(1)}, bf16[768]{0:T(1024)(128)(2,1)S(1)}, bf...) fusion(bf16[18,1,768]{2,1,0:T(2,128)(2,1)} %collective-permute-, ...), kind=kOutput, calls=%fused_computation.44 | convolution fusion | flops 625599744 | bytes 8523264 | tf_op jit(solution)/shard_map/dot_general | solution.py:87
  112.9 8.3 %fusion.2 = bf16[16,148480]{1,0:T(8,128)(2,1)} fusion(bf16[16,432]{1,0:T(8,128)(2,1)S(1)} %reshape.182, bf16[16,147456]{1,0:T(8,128)(2,1)} %reshape.181), kind=kLoop, calls=%fused_computation.3 | loop fusion | flops 16629760 | bytes 9483776 | tf_op jit(solution)/shard_map/concatenate | solution.py:65
  121.2 5.3 %reshape.183 = bf16[18560,128]{1,0:T(8,128)(2,1)} reshape(bf16[16,148480]{1,0:T(8,128)(2,1)} %fusion.2) | data formatting | bytes 9502720 | tf_op jit(solution)/shard_map/reshape | solution.py:67
  128.4 151.0 %all-reduce.4.cloned.1.call-done = bf16[18560,128]{1,0:T(8,128)(2,1)} async-done(((bf16[18560,128]{1,0:T(8,128)(2,1)}), bf16[18560,128]{1,0:T(8,128)(2,1)}) %all-reduce.4.cloned.1.call-update) | async-done | bytes 4751376
  281.2 5.7 %all-to-all-start.3 = ((bf16[8,2,216]{2,1,0:T(2,128)(2,1)}), bf16[8,2,216]{2,1,0:T(2,128)(2,1)S(1)}, u32[]{:S(2)}, u32[]{:S(2)}) async-start(bf16[8,2,216]{2,1,0:T(2,128)(2,1)} %reshape.205), calls=%async_computation.3 | async-start | bytes 16384 | tf_op jit(solution)/shard_map/all_to_all | solution.py:36
  288.3 3.3 all-to-all-done.3
  293.8 5.1 %all-to-all-start.2 = ((bf16[8,768,192]{1,2,0:T(8,128)(2,1)}), bf16[8,768,192]{1,2,0:T(8,128)(2,1)S(1)}, u32[]{:S(2)}, u32[]{:S(2)}) async-start(bf16[8,768,192]{1,2,0:T(8,128)(2,1)} %broadcast_in_dim.24), calls=%async_computation.2 | async-start | bytes 4718592 | tf_op jit(solution)/shard_map/all_to_all | solution.py:36
  298.9 2.0 collective-permute-start.5
  300.9 4.7 %collective-permute-start.4 = (bf16[1,32,768]{2,1,0:T(8,128)(2,1)S(1)}, bf16[1,32,768]{2,1,0:T(8,128)(2,1)S(1)}, u32[]{:S(2)}, u32[]{:S(2)}) collective-permute-start(bf16[1,32,768]{2,1,0:T(8,128)(2,1)S(1)} %get-tuple-element.61), channel_id=1, source_target_pairs={{0,16},{16,32},{32,48},{48,64},{64,80},{80,96},{96,112},{1,17},{17... | collective-permute-start | bytes 147464 | tf_op jit(solution)/shard_map/ppermute | solution.py:25
  305.6 20.8 %collective-permute-done.5 = bf16[1,32,768]{2,1,0:T(8,128)(2,1)S(1)} collective-permute-done((bf16[1,32,768]{2,1,0:T(8,128)(2,1)S(1)}, bf16[1,32,768]{2,1,0:T(8,128)(2,1)S(1)}, u32[]{:S(2)}, u32[]{:S(2)}) %collective-permute-start.5) | collective-permute-done | bytes 49184 | tf_op jit(solution)/shard_map/ppermute | solution.py:27
  326.5 7.7 %collective-permute-start.7 = (bf16[18,1,768]{2,1,0:T(2,128)(2,1)S(1)}, bf16[18,1,768]{2,1,0:T(2,128)(2,1)S(1)}, u32[]{:S(2)}, u32[]{:S(2)}) collective-permute-start(bf16[18,1,768]{2,1,0:T(2,128)(2,1)S(1)} %get-tuple-element.58), channel_id=1, source_target_pairs={{1,0},{2,1},{3,2},{4,3},{5,4},{6,5},{7,6},{8,7},{9,8},{10,9},{11,1... | collective-permute-start | bytes 82952 | tf_op jit(solution)/shard_map/ppermute | solution.py:27
  334.3 2.1 collective-permute-start.6
  336.4 7.1 %collective-permute-done.6 = bf16[18,1,768]{2,1,0:T(2,128)(2,1)S(1)} collective-permute-done((bf16[18,1,768]{2,1,0:T(2,128)(2,1)S(1)}, bf16[18,1,768]{2,1,0:T(2,128)(2,1)S(1)}, u32[]{:S(2)}, u32[]{:S(2)}) %collective-permute-start.6) | collective-permute-done | bytes 27680 | tf_op jit(solution)/shard_map/ppermute | solution.py:25
  343.9 2.6 fusion.24
  (168 shorter events, 40.7 us)
Async XLA Ops:
  7.2 35.4 %copy-start = (bf16[768,768]{1,0:T(8,128)(2,1)S(1)}, bf16[768,768]{1,0:T(8,128)(2,1)}, u32[]{:S(2)}) copy-start(bf16[768,768]{1,0:T(8,128)(2,1)} %param.9) | copy-start | bytes 3538948
  8.1 9.1 %collective-permute-start = (bf16[1,32,768]{2,1,0:T(8,128)(2,1)S(1)}, bf16[1,32,768]{2,1,0:T(8,128)(2,1)S(1)}, u32[]{:S(2)}, u32[]{:S(2)}) collective-permute-start(bf16[1,32,768]{2,1,0:T(8,128)(2,1)S(1)} %get-tuple-element.63), channel_id=1, source_target_pairs={{0,16},{16,32},{32,48},{48,64},{64,80},{80,96},{96,112},{1,17},{17... | collective-permute-start | bytes 147464 | tf_op jit(solution)/shard_map/ppermute | solution.py:25
  11.3 6.9 %collective-permute-start.1 = (bf16[1,32,768]{2,1,0:T(8,128)(2,1)S(1)}, bf16[1,32,768]{2,1,0:T(8,128)(2,1)S(1)}, u32[]{:S(2)}, u32[]{:S(2)}) collective-permute-start(bf16[1,32,768]{2,1,0:T(8,128)(2,1)S(1)} %get-tuple-element.64), channel_id=1, source_target_pairs={{16,0},{32,16},{48,32},{64,48},{80,64},{96,80},{112,96},{17,1},{33... | collective-permute-start | bytes 147464 | tf_op jit(solution)/shard_map/ppermute | solution.py:27
  17.2 6.6 %copy-start.39 = (f32[9,768]{1,0:T(8,128)S(1)}, f32[9,768]{1,0:T(8,128)}, u32[]{:S(2)}) copy-start(f32[9,768]{1,0:T(8,128)} %param.8) | copy-start | bytes 82948
  17.2 6.6 %copy-start.25 = (bf16[1,32,768]{2,1,0:T(8,128)(2,1)}, bf16[1,32,768]{2,1,0:T(8,128)(2,1)S(1)}, u32[]{:S(2)}) copy-start(bf16[1,32,768]{2,1,0:T(8,128)(2,1)S(1)} %collective-permute-done) | copy-start | bytes 147460
  17.3 8.7 %copy-start.22 = (bf16[16,32,768]{2,1,0:T(8,128)(2,1)S(1)}, bf16[16,32,768]{2,1,0:T(8,128)(2,1)}, u32[]{:S(2)}) copy-start(bf16[16,32,768]{2,1,0:T(8,128)(2,1)} %param.13) | copy-start | bytes 2359300
  19.1 8.0 %collective-permute-start.3 = (bf16[18,1,768]{2,1,0:T(2,128)(2,1)}, bf16[18,1,768]{2,1,0:T(2,128)(2,1)}, u32[]{:S(2)}, u32[]{:S(2)}) collective-permute-start(bf16[18,1,768]{2,1,0:T(2,128)(2,1)} %get-tuple-element.59), channel_id=1, source_target_pairs={{1,0},{2,1},{3,2},{4,3},{5,4},{6,5},{7,6},{8,7},{9,8},{10,9},{11,1... | collective-permute-start | bytes 82952 | tf_op jit(solution)/shard_map/ppermute | solution.py:27
  21.9 9.4 %collective-permute-start.2 = (bf16[18,1,768]{2,1,0:T(2,128)(2,1)}, bf16[18,1,768]{2,1,0:T(2,128)(2,1)}, u32[]{:S(2)}, u32[]{:S(2)}) collective-permute-start(bf16[18,1,768]{2,1,0:T(2,128)(2,1)} %get-tuple-element.60), channel_id=1, source_target_pairs={{0,1},{1,2},{2,3},{3,4},{4,5},{5,6},{6,7},{7,8},{8,9},{9,10},{10,1... | collective-permute-start | bytes 82952 | tf_op jit(solution)/shard_map/ppermute | solution.py:25
  36.5 7.8 %copy-start.10 = (bf16[16,32,768]{2,1,0:T(8,128)(2,1)}, bf16[16,32,768]{2,1,0:T(8,128)(2,1)S(1)}, u32[]{:S(2)}) copy-start(bf16[16,32,768]{2,1,0:T(8,128)(2,1)S(1)} %fusion.33) | copy-start | bytes 2359300
  36.7 5.9 %copy-start.20 = (f32[2,4,768]{2,1,0:T(4,128)}, f32[2,4,768]{2,1,0:T(4,128)S(1)}, u32[]{:S(2)}) copy-start(f32[2,4,768]{2,1,0:T(4,128)S(1)} %convert_reduce_fusion.1) | copy-start | bytes 73732
  37.8 10.6 %all-to-all-start = ((bf16[16,2,4,768]{3,2,1,0:T(4,128)(2,1)}), bf16[16,2,4,768]{3,2,1,0:T(4,128)(2,1)}, u32[]{:S(2)}, u32[]{:S(2)}) async-start(bf16[16,2,4,768]{3,2,1,0:T(4,128)(2,1)} %broadcast_in_dim.21), calls=%async_computation | async-start | bytes 393216 | tf_op jit(solution)/shard_map/all_to_all | solution.py:36
  64.9 8.8 %copy-start.8 = (f32[12,64,128]{2,1,0:T(8,128)S(1)}, f32[12,64,128]{2,1,0:T(8,128)}, u32[]{:S(2)}) copy-start(f32[12,64,128]{2,1,0:T(8,128)} %fusion.47) | copy-start | bytes 1179652
  64.9 8.8 %copy-start.15 = (bf16[128,768,1]{1,0,2:T(8,128)(2,1)S(1)}, bf16[128,768,1]{1,0,2:T(8,128)(2,1)}, u32[]{:S(2)}) copy-start(bf16[128,768,1]{1,0,2:T(8,128)(2,1)} %reshape.192) | copy-start | bytes 589828
  66.3 8.5 %copy-start.9 = (f32[12,64,128]{2,1,0:T(8,128)S(1)}, f32[12,64,128]{2,1,0:T(8,128)}, u32[]{:S(2)}) copy-start(f32[12,64,128]{2,1,0:T(8,128)} %fusion.45) | copy-start | bytes 1179652
  67.1 37.2 %all-to-all-start.1 = ((bf16[16,2,4,768]{3,2,1,0:T(4,128)(2,1)}), bf16[16,2,4,768]{3,2,1,0:T(4,128)(2,1)S(1)}, u32[]{:S(2)}, u32[]{:S(2)}) async-start(bf16[16,2,4,768]{3,2,1,0:T(4,128)(2,1)} %bitcast.94), calls=%async_computation.1 | async-start | bytes 393216 | tf_op jit(solution)/shard_map/all_to_all | solution.py:58
  73.6 205.8 %all-reduce.4.cloned.1.call-start = ((), (), s32[]{:S(2)}) async-start(), calls=%async_computation.4 | async-start | bytes 9502720
  93.4 11.1 %copy-start.21 = (f32[2,4,768]{2,1,0:T(4,128)S(1)}, f32[2,4,768]{2,1,0:T(4,128)}, u32[]{:S(2)}) copy-start(f32[2,4,768]{2,1,0:T(4,128)} %copy-done.20) | copy-start | bytes 73732
  93.4 11.1 %copy-start.36 = (f32[2,4]{1,0:T(2,128)S(1)}, f32[2,4]{1,0:T(2,128)}, u32[]{:S(2)}) copy-start(f32[2,4]{1,0:T(2,128)} %copy-done.35) | copy-start | bytes 100
  93.4 11.1 %copy-start.38 = (f32[2,4]{1,0:T(2,128)S(1)}, f32[2,4]{1,0:T(2,128)}, u32[]{:S(2)}) copy-start(f32[2,4]{1,0:T(2,128)} %copy-done.37) | copy-start | bytes 100
  281.2 10.5 %all-to-all-start.3 = ((bf16[8,2,216]{2,1,0:T(2,128)(2,1)}), bf16[8,2,216]{2,1,0:T(2,128)(2,1)S(1)}, u32[]{:S(2)}, u32[]{:S(2)}) async-start(bf16[8,2,216]{2,1,0:T(2,128)(2,1)} %reshape.205), calls=%async_computation.3 | async-start | bytes 16384 | tf_op jit(solution)/shard_map/all_to_all | solution.py:36
  293.8 55.5 %all-to-all-start.2 = ((bf16[8,768,192]{1,2,0:T(8,128)(2,1)}), bf16[8,768,192]{1,2,0:T(8,128)(2,1)S(1)}, u32[]{:S(2)}, u32[]{:S(2)}) async-start(bf16[8,768,192]{1,2,0:T(8,128)(2,1)} %broadcast_in_dim.24), calls=%async_computation.2 | async-start | bytes 4718592 | tf_op jit(solution)/shard_map/all_to_all | solution.py:36
  298.9 27.5 %collective-permute-start.5 = (bf16[1,32,768]{2,1,0:T(8,128)(2,1)S(1)}, bf16[1,32,768]{2,1,0:T(8,128)(2,1)S(1)}, u32[]{:S(2)}, u32[]{:S(2)}) collective-permute-start(bf16[1,32,768]{2,1,0:T(8,128)(2,1)S(1)} %get-tuple-element.62), channel_id=1, source_target_pairs={{16,0},{32,16},{48,32},{64,48},{80,64},{96,80},{112,96},{17,1},{33... | collective-permute-start | bytes 147464 | tf_op jit(solution)/shard_map/ppermute | solution.py:27
  300.9 25.5 %collective-permute-start.4 = (bf16[1,32,768]{2,1,0:T(8,128)(2,1)S(1)}, bf16[1,32,768]{2,1,0:T(8,128)(2,1)S(1)}, u32[]{:S(2)}, u32[]{:S(2)}) collective-permute-start(bf16[1,32,768]{2,1,0:T(8,128)(2,1)S(1)} %get-tuple-element.61), channel_id=1, source_target_pairs={{0,16},{16,32},{32,48},{48,64},{64,80},{80,96},{96,112},{1,17},{17... | collective-permute-start | bytes 147464 | tf_op jit(solution)/shard_map/ppermute | solution.py:25
  326.5 9.9 %collective-permute-start.7 = (bf16[18,1,768]{2,1,0:T(2,128)(2,1)S(1)}, bf16[18,1,768]{2,1,0:T(2,128)(2,1)S(1)}, u32[]{:S(2)}, u32[]{:S(2)}) collective-permute-start(bf16[18,1,768]{2,1,0:T(2,128)(2,1)S(1)} %get-tuple-element.58), channel_id=1, source_target_pairs={{1,0},{2,1},{3,2},{4,3},{5,4},{6,5},{7,6},{8,7},{9,8},{10,9},{11,1... | collective-permute-start | bytes 82952 | tf_op jit(solution)/shard_map/ppermute | solution.py:27
  334.2 9.6 %copy-start.17 = (f32[16,32,768]{2,1,0:T(8,128)S(1)}, f32[16,32,768]{2,1,0:T(8,128)}, u32[]{:S(2)}) copy-start(f32[16,32,768]{2,1,0:T(8,128)} %get-tuple-element.69) | copy-start | bytes 4718596
  334.2 9.6 %copy-start.29 = (f32[768]{0:T(1024)S(1)}, f32[768]{0:T(1024)}, u32[]{:S(2)}) copy-start(f32[768]{0:T(1024)} %get-tuple-element.51) | copy-start | bytes 9220
  334.2 9.6 %copy-start.30 = (f32[768]{0:T(1024)S(1)}, f32[768]{0:T(1024)}, u32[]{:S(2)}) copy-start(f32[768]{0:T(1024)} %get-tuple-element.52) | copy-start | bytes 9220
  334.3 9.6 %copy-start.31 = (f32[768]{0:T(1024)S(1)}, f32[768]{0:T(1024)}, u32[]{:S(2)}) copy-start(f32[768]{0:T(1024)} %get-tuple-element.53) | copy-start | bytes 9220
  334.3 9.6 %copy-start.32 = (f32[768]{0:T(1024)S(1)}, f32[768]{0:T(1024)}, u32[]{:S(2)}) copy-start(f32[768]{0:T(1024)} %get-tuple-element.54) | copy-start | bytes 9220
  334.3 9.6 %copy-start.33 = (f32[768]{0:T(1024)S(1)}, f32[768]{0:T(1024)}, u32[]{:S(2)}) copy-start(f32[768]{0:T(1024)} %get-tuple-element.55) | copy-start | bytes 9220
  334.3 9.2 %collective-permute-start.6 = (bf16[18,1,768]{2,1,0:T(2,128)(2,1)S(1)}, bf16[18,1,768]{2,1,0:T(2,128)(2,1)S(1)}, u32[]{:S(2)}, u32[]{:S(2)}) collective-permute-start(bf16[18,1,768]{2,1,0:T(2,128)(2,1)S(1)} %get-tuple-element.57), channel_id=1, source_target_pairs={{0,1},{1,2},{2,3},{3,4},{4,5},{5,6},{6,7},{7,8},{8,9},{9,10},{10,1... | collective-permute-start | bytes 82952 | tf_op jit(solution)/shard_map/ppermute | solution.py:25
  343.9 6.5 %copy-start.1 = (bf16[768,768]{1,0:T(8,128)(2,1)S(1)}, bf16[768,768]{1,0:T(8,128)(2,1)}, u32[]{:S(2)}) copy-start(bf16[768,768]{1,0:T(8,128)(2,1)} %param.9) | copy-start | bytes 3538948
  (22 other events, 59.8 us)
Sparse Core Ops, SparseCore 0:
  126.6 152.7 all-reduce.3
where the time goes:
time: 359 us; the launch traced here: 357 us
  waiting for transfers between devices  190 us (53%)
  local copies, waits for them, and re-layouts  50.8 us (14%)
  starting transfers between devices  49.2 us (14%)
  matrix products  28.9 us (8%)
  other arithmetic  23 us (6%)
  between operations  15.4 us (4%)
    unnamed x2, waiting for transfers between devices  151 us
    ppermute x4, waiting for transfers between devices, with_halo(): lax.ppermute(head, axis, [((i + 1) % count, i) for i in range(ends)])  21.6 us
    all_to_all x3, starting transfers between devices, copy_for_each(): lax.all_to_all(jnp.broadcast_to(x[None], (peers, *x.shape)), axis, 0, 0,...  15.6 us
    ppermute x4, starting transfers between devices, with_halo(): lax.ppermute(head, axis, [((i + 1) % count, i) for i in range(ends)])  15.1 us
    ppermute x4, starting transfers between devices, with_halo(): lax.ppermute(tail, axis, [(i, (i + 1) % count) for i in range(ends)])  11.9 us
    ppermute x4, waiting for transfers between devices, with_halo(): lax.ppermute(tail, axis, [(i, (i + 1) % count) for i in range(ends)])  11.3 us
    reshape x2, local copies, waits for them, and re-layouts, sum_together(): lines = jnp.concatenate([b.reshape(peers, -1) for b in parts], axis=1)  11 us
    dot_general x2, matrix products, contract_last(): lax.dot_general(left, right, (((1,), (1,)), ((), ())), preferred_element_...  9.41 us
  transfers between devices with their start and end apart: 13, of which 7 were waited for; matrix products, arithmetic and copies ran while one was open for 13% of the time, Pallas kernels for 0%

commit v1 on v0

v1 whole, which is shorter than its diff:
```python
from functools import partial
import math

import jax
import jax.numpy as jnp
from jax import lax
from jax.sharding import PartitionSpec as P

HEADS = 12
HD = 64
POOL = 8
EPSILON = 1e-05
BF = jnp.bfloat16
F32 = jnp.float32

FINAL = (0, 1, 2, 3, 12, 13, 14, 15)
PARTNER = (5, 4, 7, 6, 9, 8, 11, 10)
SLICE_AT = tuple((FINAL.index(j) if j in FINAL else PARTNER.index(j)) for j in range(16))
PAIRS = [(j, j ^ 1) for j in range(16)]


def holder(piece, core):
    return FINAL[piece] if FINAL[piece] % 2 == core else PARTNER[piece]


SUM_GROUPS = [[q * 16 + holder(s, c) for s in range(8) for q in range(8)] for c in range(2)]
PLACE_GROUPS = [[q * 16 + holder(s, c) for c in range(2) for q in range(8)] for s in range(8)]
BOTH = ("row", "col")


def with_halo(cells, sides, width):
    for axis, dim in sides:
        count = lax.axis_size(axis)
        ends = count - 1
        head = lax.slice_in_dim(cells, 0, width, axis=dim)
        tail = lax.slice_in_dim(cells, cells.shape[dim] - width, cells.shape[dim], axis=dim)
        cells = jnp.concatenate(
            [
                lax.ppermute(tail, axis, [(i, (i + 1) % count) for i in range(ends)]),
                cells,
                lax.ppermute(head, axis, [((i + 1) % count, i) for i in range(ends)]),
            ],
            axis=dim,
        )
    return cells


def copy_for_each(x, axis):
    peers = lax.axis_size(axis)
    return lax.all_to_all(jnp.broadcast_to(x[None], (peers, *x.shape)), axis, 0, 0, tiled=True)


def contract_first(left, right):
    return lax.dot_general(left, right, (((0,), (0,)), ((), ())), preferred_element_type=F32)


def contract_last(left, right):
    return lax.dot_general(left, right, (((1,), (1,)), ((), ())), preferred_element_type=F32)


def stencil(padded, taps, height, width, flipped):
    total = jnp.zeros((height, width, padded.shape[2]), F32)
    for tap_row in range(3):
        for tap_col in range(3):
            if flipped:
                window = padded[
                    2 - tap_row : 2 - tap_row + height, 2 - tap_col : 2 - tap_col + width
                ]
            else:
                window = padded[tap_row : tap_row + height, tap_col : tap_col + width]
            total = total + taps[3 * tap_row + tap_col] * window.astype(F32)
    return total


def attend(query, dout, keys, values):
    scale = HD ** (-0.5)
    q = query.reshape(-1, HEADS, HD)
    d = dout.reshape(-1, HEADS, HD)
    k = keys.reshape(-1, HEADS, HD)
    v = values.reshape(-1, HEADS, HD)
    scores = jnp.einsum("qhd,khd->hqk", q, k, preferred_element_type=F32) * scale
    expons = jnp.exp(scores)
    probs = expons / jnp.sum(expons, axis=-1, keepdims=True)
    weights = probs.astype(BF)
    attended = jnp.einsum("hqk,khd->qhd", weights, v, preferred_element_type=F32).astype(BF)
    grad_probs = jnp.einsum("qhd,khd->hqk", d, v, preferred_element_type=F32)
    deltas = jnp.einsum("qhd,qhd->hq", d, attended, preferred_element_type=F32)
    grad_scores = (probs * (grad_probs - deltas[:, :, None]) * scale).astype(BF)
    grad_query = jnp.einsum("hqk,khd->qhd", grad_scores, k, preferred_element_type=F32).astype(BF)
    grad_key = jnp.einsum("hqk,qhd->khd", grad_scores, q, preferred_element_type=F32)
    grad_value = jnp.einsum("hqk,qhd->khd", weights, d, preferred_element_type=F32)
    n = query.shape[1]
    return (
        attended.reshape(-1, n),
        grad_query.reshape(-1, n),
        grad_key.reshape(-1, n).astype(BF),
        grad_value.reshape(-1, n).astype(BF),
    )


def on_device(image, conv_taps, w_query, w_key, w_value, w_out, grad_out):
    height, width, channels = image.shape
    half = channels // 2
    at_row, at_col = lax.axis_index("row"), lax.axis_index("col")
    core = at_col % 2
    flat_grad = grad_out.reshape(-1, channels)
    padded = with_halo(image, (("row", 0), ("col", 1)), 1)
    dout = contract_last(flat_grad, w_out).astype(BF)
    hidden = (image.astype(F32) + stencil(padded, conv_taps, height, width, False)).astype(BF)
    flat_hidden = hidden.reshape(-1, channels)
    pooled = (
        hidden.astype(F32)
        .reshape(height // POOL, POOL, width // POOL, POOL, channels)
        .mean(axis=(1, 3))
        .reshape(-1, channels)
    )
    centre = jnp.mean(pooled, axis=-1, keepdims=True)
    spread = jnp.mean(jnp.square(pooled - centre), axis=-1, keepdims=True)
    inverse = lax.rsqrt(spread + EPSILON)
    standard = (pooled - centre) * inverse
    n_own = standard.shape[0]
    cells = copy_for_each(standard.astype(BF), "col").reshape(-1, channels)
    query = jnp.dot(flat_hidden, w_query, preferred_element_type=F32).astype(BF)
    keys = jnp.dot(cells, w_key, preferred_element_type=F32).astype(BF)
    values = jnp.dot(cells, w_value, preferred_element_type=F32).astype(BF)
    cells_half = lax.dynamic_slice_in_dim(cells, core * half, half, axis=1)
    all_cells = copy_for_each(cells_half, "row").reshape(-1, half)
    attended, grad_query, grad_key, grad_value = attend(query, dout, keys, values)
    terms = jnp.concatenate([grad_key, grad_value], axis=1).reshape(16, n_own, 2 * channels)
    terms = lax.all_to_all(terms, "col", 0, 0, tiled=True)
    def half_terms(which):
        h = lax.dynamic_slice_in_dim(flat_hidden, which * half, half, axis=1)
        a = lax.dynamic_slice_in_dim(attended, which * half, half, axis=1)
        return jnp.concatenate([contract_first(grad_query, h), contract_first(flat_grad, a)], axis=0)

    theirs = lax.ppermute(half_terms(1 - core).astype(BF), "col", PAIRS)
    chip = (half_terms(core) + theirs.astype(F32)).astype(BF)
    got = lax.all_to_all(
        chip.reshape(64, 24, half), BOTH, 0, 0, tiled=True, axis_index_groups=SUM_GROUPS
    )
    grad_hidden = contract_last(grad_query, w_query)
    early = grad_out.astype(F32) + grad_hidden.reshape(height, width, channels)
    sums = jnp.sum(terms.astype(F32), axis=0)
    sums_bf = sums.astype(BF)
    grad_normed = contract_last(sums_bf[:, :channels], w_key) + contract_last(
        sums_bf[:, channels:], w_value
    )
    grad_pooled = (
        grad_normed
        - jnp.mean(grad_normed, axis=-1, keepdims=True)
        - standard * jnp.mean(grad_normed * standard, axis=-1, keepdims=True)
    ) * inverse
    spread_back = jnp.broadcast_to(
        (grad_pooled / (POOL * POOL)).reshape(height // POOL, 1, width // POOL, 1, channels),
        (height // POOL, POOL, width // POOL, POOL, channels),
    ).reshape(height, width, channels)
    grad_mixed = early + spread_back
    tap_list = []
    for tap_row in range(3):
        for tap_col in range(3):
            window = padded[tap_row : tap_row + height, tap_col : tap_col + width]
            tap_list.append(jnp.sum(grad_mixed * window.astype(F32), axis=(0, 1)))
    tap_terms = jnp.stack(tap_list, axis=0).astype(BF)
    kv = jnp.transpose(sums_bf.reshape(n_own, 8, 8, 24), (2, 1, 0, 3))
    kv = jnp.concatenate([kv[:, PARTNER[SLICE_AT[j]] - 4][:, None] for j in range(16)], axis=1)
    taps = jnp.transpose(tap_terms.reshape(9, 16, 48), (1, 0, 2))
    last = jnp.pad(taps[:, 8:], ((0, 0), (0, 7), (0, 0)))
    taps = jnp.broadcast_to(jnp.concatenate([taps[:, :8], last], axis=2)[None], (8, 16, 8, 96))
    block = jnp.pad(jnp.concatenate([kv, taps], axis=3), ((0, 0), (0, 0), (0, 0), (0, 8)))
    blocks = lax.all_to_all(block.reshape(128, 8, 128), BOTH, 0, 0, tiled=True)
    kv_piece = contract_first(blocks.reshape(1024, 128), all_cells)[:24].astype(BF)
    tap_sums = jnp.sum(blocks.astype(F32), axis=0)
    grad_conv = jnp.concatenate([tap_sums[:, 24:72], tap_sums[:1, 72:120]], axis=0)
    piece = jnp.sum(got.astype(F32), axis=0).astype(BF)
    parity = (at_col % 2) ^ ((at_col >= 4) & (at_col < 12)).astype(at_col.dtype)
    first = jnp.where(parity == 0, piece, kv_piece)
    second = jnp.where(parity == 0, kv_piece, piece)
    placed = jnp.broadcast_to(jnp.stack([first, second])[:, None], (2, 8, 24, half))
    placed = lax.all_to_all(
        placed.reshape(16, 24, half), BOTH, 0, 0, tiled=True, axis_index_groups=PLACE_GROUPS
    )
    grad_weights = jnp.transpose(placed.reshape(2, 192, half), (0, 2, 1)).reshape(channels, 192)
    grad_padded = with_halo(grad_mixed.astype(BF), (("row", 0), ("col", 1)), 1)
    grad_image = (grad_mixed + stencil(grad_padded, conv_taps, height, width, True)).astype(BF)
    return (grad_image, grad_weights.astype(F32), grad_conv)


def solution(mesh):
    return jax.shard_map(
        on_device,
        mesh=mesh,
        in_specs=(P("row", "col", None), P(), P(), P(), P(), P(), P("row", "col", None)),
        out_specs=(P("row", "col", None), P(None, "col"), P(None, "col")),
        check_vma=False,
    )
```

time: 359 us -> 228 us (0.64)
  waiting for transfers between devices: 190 us -> 42.8 us
  between operations: 15.4 us -> 1.23 us
  starting transfers between devices: 49.2 us -> 63.3 us
  local copies, waits for them, and re-layouts: 50.8 us -> 56.5 us
  matrix products: 28.9 us -> 34.3 us
    unnamed x2 -> x0, waiting for transfers between devices: 151 us -> none
    all_to_all x1 -> x4, starting transfers between devices: 6.51 us -> 31.6 us  [the longest x1 9.82 us: on_device(): blocks = lax.all_to_all(block.reshape(128, 8, 128), BOTH, 0, 0, tiled=True)]
    reshape x4 -> x1, local copies, waits for them, and re-layouts: 17.2 us -> 1.6 us  [on_device(): kv = jnp.transpose(sums_bf.reshape(n_own, 8, 8, 24), (2, 1, 0, 3))]
    unnamed x95 -> x68, local copies, waits for them, and re-layouts: 5.47 us -> 18.1 us
    ppermute x4, waiting for transfers between devices: 21.6 us -> 12.1 us  [with_halo(): lax.ppermute(head, axis, [((i + 1) % count, i) for i in range(ends)])]
    transpose x3 -> x0, local copies, waits for them, and re-layouts: 8.96 us -> none  [the longest x2 7.96 us: cut_along(): return jnp.moveaxis(parts, dim, 0)]
    another operation x12 -> x10, local copies, waits for them, and re-layouts: 2.61 us -> 10.3 us  [on_device(): tap_terms = jnp.stack(tap_list, axis=0).astype(BF)]
    all_to_all x1 -> x4, waiting for transfers between devices: 0.01 us -> 6.86 us  [the longest x1 5.37 us: on_device(): blocks = lax.all_to_all(block.reshape(128, 8, 128), BOTH, 0, 0, tiled=True)]
  transfers between devices with their start and end apart: 13 -> 15, of which waited for: 7 -> 8; matrix products, arithmetic and copies ran while one was open for 13% -> 36% of each run, Pallas kernels for 0% -> 0%
where the time goes in v1:
time: 228 us; the launch traced here: 224 us
  starting transfers between devices  63.3 us (28%)
  local copies, waits for them, and re-layouts  56.5 us (25%)
  waiting for transfers between devices  42.8 us (19%)
  matrix products  34.3 us (15%)
  other arithmetic  26 us (11%)
    unnamed x68, local copies, waits for them, and re-layouts  18.1 us
    ppermute x4, waiting for transfers between devices, with_halo(): lax.ppermute(tail, axis, [(i, (i + 1) % count) for i in range(ends)])  13.2 us
    dot_general x4, matrix products, contract_last(): lax.dot_general(left, right, (((1,), (1,)), ((), ())), preferred_element_...  13 us
    ppermute x4, waiting for transfers between devices, with_halo(): lax.ppermute(head, axis, [((i + 1) % count, i) for i in range(ends)])  12.1 us
    ppermute x4, starting transfers between devices, with_halo(): lax.ppermute(tail, axis, [(i, (i + 1) % count) for i in range(ends)])  11.5 us
    all_to_all x2, waiting for transfers between devices, copy_for_each(): lax.all_to_all(jnp.broadcast_to(x[None], (peers, *x.shape)), axis, 0, 0,...  10.5 us
    another operation x10, local copies, waits for them, and re-layouts, on_device(): tap_terms = jnp.stack(tap_list, axis=0).astype(BF)  10.3 us
    all_to_all x2, starting transfers between devices, copy_for_each(): lax.all_to_all(jnp.broadcast_to(x[None], (peers, *x.shape)), axis, 0, 0,...  10.1 us
  transfers between devices with their start and end apart: 15, of which 8 were waited for; matrix products, arithmetic and copies ran while one was open for 36% of the time, Pallas kernels for 0%

profile of v1, /device:TPU:96, one launch (start us, length us, event | category | flops | bytes accessed | tf_op | source)
XLA Modules:
  0.0 224.2 jit_solution(330283199263106788)
XLA Ops:
  1.6 3.2 %collective-permute-start = (bf16[1,32,768]{2,1,0:T(8,128)(2,1)S(1)}, bf16[1,32,768]{2,1,0:T(8,128)(2,1)S(1)}, u32[]{:S(2)}, u32[]{:S(2)}) collective-permute-start(bf16[1,32,768]{2,1,0:T(8,128)(2,1)S(1)} %get-tuple-element.38), channel_id=1, source_target_pairs={{0,16},{16,32},{32,48},{48,64},{64,80},{80,96},{96,112},{1,17},{17... | collective-permute-start | bytes 147464 | tf_op jit(solution)/shard_map/ppermute | solution.py:39
  4.8 2.6 %collective-permute-start.1 = (bf16[1,32,768]{2,1,0:T(8,128)(2,1)S(1)}, bf16[1,32,768]{2,1,0:T(8,128)(2,1)S(1)}, u32[]{:S(2)}, u32[]{:S(2)}) collective-permute-start(bf16[1,32,768]{2,1,0:T(8,128)(2,1)S(1)} %get-tuple-element.39), channel_id=1, source_target_pairs={{16,0},{32,16},{48,32},{64,48},{80,64},{96,80},{112,96},{17,1},{33... | collective-permute-start | bytes 147464 | tf_op jit(solution)/shard_map/ppermute | solution.py:41
  7.4 2.4 %convolution_convert_fusion = bf16[512,768]{1,0:T(8,128)(2,1)S(1)} fusion(bf16[512,768]{1,0:T(8,128)(2,1)} %bitcast.101, bf16[768,768]{1,0:T(8,128)(2,1)} %param.12), kind=kOutput, calls=%fused_computation.53 | convolution fusion | flops 604372992 | bytes 2752512 | tf_op jit(solution)/shard_map/dot_general | solution.py:58
  13.4 2.6 %collective-permute-start.3 = (bf16[18,1,768]{2,1,0:T(2,128)(2,1)}, bf16[18,1,768]{2,1,0:T(2,128)(2,1)}, u32[]{:S(2)}, u32[]{:S(2)}) collective-permute-start(bf16[18,1,768]{2,1,0:T(2,128)(2,1)} %get-tuple-element.34), channel_id=1, source_target_pairs={{1,0},{2,1},{3,2},{4,3},{5,4},{6,5},{7,6},{8,7},{9,8},{10,9},{11,1... | collective-permute-start | bytes 82952 | tf_op jit(solution)/shard_map/ppermute | solution.py:41
  16.0 1.9 collective-permute-start.2
  18.9 6.5 %collective-permute-done.2 = bf16[18,1,768]{2,1,0:T(2,128)(2,1)} collective-permute-done((bf16[18,1,768]{2,1,0:T(2,128)(2,1)}, bf16[18,1,768]{2,1,0:T(2,128)(2,1)}, u32[]{:S(2)}, u32[]{:S(2)}) %collective-permute-start.2) | collective-permute-done | bytes 27680 | tf_op jit(solution)/shard_map/ppermute | solution.py:39
  25.4 5.4 %fusion.21 = bf16[16,32,768]{2,1,0:T(8,128)(2,1)S(1)} fusion(bf16[16,32,768]{2,1,0:T(8,128)(2,1)S(1)} %copy-done.3, bf16[1,32,768]{2,1,0:T(8,128)(2,1)} %copy-done.14, bf16[1,32,768]{2,1,0:T(8,128)(2,1)} %copy-done.13, f32[768]{0:T(1024)} %get-tuple-element.25, f32[768]{0:T(1024)} %get-tuple-element.26, f32[768]{0:T(1024)S(1)} %get-tuple-element.19, ...), kind=kLoop, calls=%fused_computation.47 | loop fusion | flops 20447232 | bytes 2638848 | tf_op jit(solution)/shard_map/convert_element_type | solution.py:109
  32.2 4.8 %all-to-all-start = ((bf16[16,8,768]{2,1,0:T(8,128)(2,1)}), bf16[16,8,768]{2,1,0:T(8,128)(2,1)}, u32[]{:S(2)}, u32[]{:S(2)}) async-start(bf16[16,8,768]{2,1,0:T(8,128)(2,1)} %broadcast_in_dim.12), calls=%async_computation | async-start | bytes 393216 | tf_op jit(solution)/shard_map/all_to_all | solution.py:50
  40.1 2.7 %all-to-all-done = bf16[16,8,768]{2,1,0:T(8,128)(2,1)} async-done(((bf16[16,8,768]{2,1,0:T(8,128)(2,1)}), bf16[16,8,768]{2,1,0:T(8,128)(2,1)}, u32[]{:S(2)}, u32[]{:S(2)}) %all-to-all-start) | async-done | bytes 196640 | tf_op jit(solution)/shard_map/all_to_all | solution.py:50
  42.8 2.4 %convolution_convert_fusion.9 = bf16[128,768]{1,0:T(8,128)(2,1)} fusion(bf16[768,768]{1,0:T(8,128)(2,1)} %param.10, bf16[16,8,768]{2,1,0:T(8,128)(2,1)} %all-to-all-done), kind=kOutput, calls=%fused_computation.65 | convolution fusion | flops 151093248 | bytes 1572864 | tf_op jit(solution)/shard_map/dot_general | solution.py:124
  46.9 2.4 %convolution_convert_fusion.8 = bf16[128,768]{1,0:T(8,128)(2,1)} fusion(bf16[768,768]{1,0:T(8,128)(2,1)} %param.11, bf16[16,8,768]{2,1,0:T(8,128)(2,1)} %all-to-all-done), kind=kOutput, calls=%fused_computation.64 | convolution fusion | flops 151093248 | bytes 1572864 | tf_op jit(solution)/shard_map/dot_general | solution.py:125
  64.0 7.0 %all-to-all-start.1 = ((bf16[16,8,1536]{2,1,0:T(8,128)(2,1)}), bf16[16,8,1536]{2,1,0:T(8,128)(2,1)}, u32[]{:S(2)}, u32[]{:S(2)}) async-start(bf16[16,8,1536]{2,1,0:T(8,128)(2,1)} %pad_maximum_fusion.8), calls=%async_computation.1 | async-start | bytes 786432 | tf_op jit(solution)/shard_map/all_to_all | solution.py:130
  71.0 2.9 %copy.83 = bf16[512,12,64]{2,1,0:T(8,128)(2,1)} copy(bf16[512,12,64]{0,2,1:T(8,128)(2,1)S(1)} %bitcast.88) | data formatting | bytes 1572864 | tf_op jit(solution)/shard_map/convert_element_type | solution.py:89
  73.8 3.9 %dot_general.72 = bf16[16,32,768]{2,1,0:T(8,128)(2,1)} reshape(bf16[512,12,64]{2,1,0:T(8,128)(2,1)} %copy.83) | data formatting | bytes 1572864 | tf_op jit(solution)/shard_map/dot_general | solution.py:58
  85.6 1.9 fusion.54
  88.8 7.0 %fusion.18 = (bf16[768]{0:T(1024)(128)(2,1)}, bf16[768]{0:T(1024)(128)(2,1)}, bf16[768]{0:T(1024)(128)(2,1)}, bf16[768]{0:T(1024)(128)(2,1)}, bf16[768]{0:T(1024...) fusion(bf16[18,1,768]{2,1,0:T(2,128)(2,1)} %collective-permute-, ...), kind=kOutput, calls=%fused_computation.40 | convolution fusion | flops 625599744 | bytes 8523264 | tf_op jit(solution)/shard_map/dot_general | solution.py:58
  127.2 9.8 %all-to-all-start.3 = ((bf16[128,8,128]{2,1,0:T(8,128)(2,1)}), bf16[128,8,128]{2,1,0:T(8,128)(2,1)}, u32[]{:S(2)}, u32[]{:S(2)}) async-start(bf16[128,8,128]{2,1,0:T(8,128)(2,1)} %bitcast.118), calls=%async_computation.3 | async-start | bytes 524288 | tf_op jit(solution)/shard_map/all_to_all | solution.py:170
  137.0 2.9 %convolution_bitcast_fusion = f32[768,384]{1,0:T(8,128)} fusion(bf16[512,768]{1,0:T(8,128)(2,1)} %bitcast.102, bf16[512,768]{0,1:T(8,128)(2,1)} %bitcast.105, s32[]{:T(128)S(6)} %select_n.32), kind=kOutput, calls=%fused_computation.52 | convolution fusion | flops 301989888 | bytes 2359300 | tf_op jit(solution)/shard_map/dot_general | solution.py:54
  140.0 5.4 %all-to-all-done.3 = bf16[128,8,128]{2,1,0:T(8,128)(2,1)} async-done(((bf16[128,8,128]{2,1,0:T(8,128)(2,1)}), bf16[128,8,128]{2,1,0:T(8,128)(2,1)}, u32[]{:S(2)}, u32[]{:S(2)}) %all-to-all-start.3) | async-done | bytes 262176 | tf_op jit(solution)/shard_map/all_to_all | solution.py:170
  147.2 5.3 %all-to-all-start.4 = ((bf16[8,128,384]{2,1,0:T(8,128)(2,1)}), bf16[8,128,384]{2,1,0:T(8,128)(2,1)}, u32[]{:S(2)}, u32[]{:S(2)}) async-start(bf16[8,128,384]{2,1,0:T(8,128)(2,1)} %broadcast_in_dim.16), calls=%async_computation.4 | async-start | bytes 1572864 | tf_op jit(solution)/shard_map/all_to_all | solution.py:50
  153.8 2.6 %fusion.2 = bf16[1536,384]{1,0:T(8,128)(2,1)} fusion(f32[768,384]{1,0:T(8,128)S(1)} %copy-done.2, f32[768,384]{1,0:T(8,128)S(1)} %fusion.36, bf16[1536,384]{1,0:T(8,128)(2,1)} %collective-permute-done.8), kind=kLoop, calls=%fused_computation.8 | loop fusion | flops 2359296 | bytes 4718592 | tf_op jit(solution)/shard_map/convert_element_type | solution.py:137
  156.4 7.8 %all-to-all-done.4 = bf16[8,128,384]{2,1,0:T(8,128)(2,1)} async-done(((bf16[8,128,384]{2,1,0:T(8,128)(2,1)}), bf16[8,128,384]{2,1,0:T(8,128)(2,1)}, u32[]{:S(2)}, u32[]{:S(2)}) %all-to-all-start.4) | async-done | bytes 786464 | tf_op jit(solution)/shard_map/all_to_all | solution.py:50
  164.2 7.9 %all-to-all-start.2 = ((bf16[64,24,384]{2,1,0:T(8,128)(2,1)}), bf16[64,24,384]{2,1,0:T(8,128)(2,1)}, u32[]{:S(2)}, u32[]{:S(2)}) async-start(bf16[64,24,384]{2,1,0:T(8,128)(2,1)} %bitcast.100), calls=%async_computation.2 | async-start | bytes 2359296 | tf_op jit(solution)/shard_map/all_to_all | solution.py:138
  172.1 2.8 %collective-permute-start.5 = (bf16[1,32,768]{2,1,0:T(8,128)(2,1)S(1)}, bf16[1,32,768]{2,1,0:T(8,128)(2,1)S(1)}, u32[]{:S(2)}, u32[]{:S(2)}) collective-permute-start(bf16[1,32,768]{2,1,0:T(8,128)(2,1)S(1)} %get-tuple-element.37), channel_id=1, source_target_pairs={{16,0},{32,16},{48,32},{64,48},{80,64},{96,80},{112,96},{17,1},{33... | collective-permute-start | bytes 147464 | tf_op jit(solution)/shard_map/ppermute | solution.py:41
  174.9 4.0 %collective-permute-start.4 = (bf16[1,32,768]{2,1,0:T(8,128)(2,1)S(1)}, bf16[1,32,768]{2,1,0:T(8,128)(2,1)S(1)}, u32[]{:S(2)}, u32[]{:S(2)}) collective-permute-start(bf16[1,32,768]{2,1,0:T(8,128)(2,1)S(1)} %get-tuple-element.36), channel_id=1, source_target_pairs={{0,16},{16,32},{32,48},{48,64},{64,80},{80,96},{96,112},{1,17},{17... | collective-permute-start | bytes 147464 | tf_op jit(solution)/shard_map/ppermute | solution.py:39
  178.9 10.4 %collective-permute-done.5 = bf16[1,32,768]{2,1,0:T(8,128)(2,1)S(1)} collective-permute-done((bf16[1,32,768]{2,1,0:T(8,128)(2,1)S(1)}, bf16[1,32,768]{2,1,0:T(8,128)(2,1)S(1)}, u32[]{:S(2)}, u32[]{:S(2)}) %collective-permute-start.5) | collective-permute-done | bytes 49184 | tf_op jit(solution)/shard_map/ppermute | solution.py:41
  189.4 1.9 collective-permute-start.6
  191.3 2.4 %collective-permute-start.7 = (bf16[18,1,768]{2,1,0:T(2,128)(2,1)S(1)}, bf16[18,1,768]{2,1,0:T(2,128)(2,1)}, u32[]{:S(2)}, u32[]{:S(2)}) collective-permute-start(bf16[18,1,768]{2,1,0:T(2,128)(2,1)S(1)} %get-tuple-element.33), channel_id=1, source_target_pairs={{0,1},{1,2},{2,3},{3,4},{4,5},{5,6},{6,7},{7,8},{8,9},{9,10},{10,1... | collective-permute-start | bytes 82952 | tf_op jit(solution)/shard_map/ppermute | solution.py:39
  193.7 6.8 %collective-permute-done.7 = bf16[18,1,768]{2,1,0:T(2,128)(2,1)} collective-permute-done((bf16[18,1,768]{2,1,0:T(2,128)(2,1)S(1)}, bf16[18,1,768]{2,1,0:T(2,128)(2,1)}, u32[]{:S(2)}, u32[]{:S(2)}) %collective-permute-start.7) | collective-permute-done | bytes 27680 | tf_op jit(solution)/shard_map/ppermute | solution.py:39
  202.5 2.2 fusion.39
  207.6 7.0 %all-to-all-start.5 = ((bf16[16,24,384]{2,1,0:T(8,128)(2,1)}), bf16[16,24,384]{2,1,0:T(8,128)(2,1)}, u32[]{:S(2)}, u32[]{:S(2)}) async-start(bf16[16,24,384]{2,1,0:T(8,128)(2,1)} %bitcast.117), calls=%async_computation.5 | async-start | bytes 589824 | tf_op jit(solution)/shard_map/all_to_all | solution.py:179
  214.6 4.3 %add_convert_fusion = bf16[16,32,768]{2,1,0:T(8,128)(2,1)} fusion(f32[16,32,768]{2,1,0:T(8,128)} %get-tuple-element.49, bf16[16,32,768]{2,1,0:T(8,128)(2,1)} %copy-done.1, bf16[18,33,768]{2,1,0:T(8,128)(2,1)S(1)} %get-tuple-element.31, bf16[1,32,768]{2,1,0:T(8,128)(2,1)S(1)} %collective-permute-done.4, bf16[18,33,768]{2,1,0:T(8,128)(2,1)S(1)} %get-tuple-element.30, ...), kind=kLoop, calls=%fused_computation.45 | loop fusion | flops 11796480 | bytes 7990272 | tf_op jit(solution)/shard_map/convert_element_type | solution.py:184
  (153 shorter events, 79.8 us)
Async XLA Ops:
  0.6 36.4 %copy-start = (bf16[768,768]{1,0:T(8,128)(2,1)S(1)}, bf16[768,768]{1,0:T(8,128)(2,1)}, u32[]{:S(2)}) copy-start(bf16[768,768]{1,0:T(8,128)(2,1)} %param.9) | copy-start | bytes 3538948
  1.6 8.3 %collective-permute-start = (bf16[1,32,768]{2,1,0:T(8,128)(2,1)S(1)}, bf16[1,32,768]{2,1,0:T(8,128)(2,1)S(1)}, u32[]{:S(2)}, u32[]{:S(2)}) collective-permute-start(bf16[1,32,768]{2,1,0:T(8,128)(2,1)S(1)} %get-tuple-element.38), channel_id=1, source_target_pairs={{0,16},{16,32},{32,48},{48,64},{64,80},{80,96},{96,112},{1,17},{17... | collective-permute-start | bytes 147464 | tf_op jit(solution)/shard_map/ppermute | solution.py:39
  4.8 6.9 %collective-permute-start.1 = (bf16[1,32,768]{2,1,0:T(8,128)(2,1)S(1)}, bf16[1,32,768]{2,1,0:T(8,128)(2,1)S(1)}, u32[]{:S(2)}, u32[]{:S(2)}) collective-permute-start(bf16[1,32,768]{2,1,0:T(8,128)(2,1)S(1)} %get-tuple-element.39), channel_id=1, source_target_pairs={{16,0},{32,16},{48,32},{64,48},{80,64},{96,80},{112,96},{17,1},{33... | collective-permute-start | bytes 147464 | tf_op jit(solution)/shard_map/ppermute | solution.py:41
  9.8 8.1 %copy-start.24 = (f32[9,768]{1,0:T(8,128)S(1)}, f32[9,768]{1,0:T(8,128)}, u32[]{:S(2)}) copy-start(f32[9,768]{1,0:T(8,128)} %param.8) | copy-start | bytes 82948
  9.8 3.5 %copy-start.13 = (bf16[1,32,768]{2,1,0:T(8,128)(2,1)}, bf16[1,32,768]{2,1,0:T(8,128)(2,1)S(1)}, u32[]{:S(2)}) copy-start(bf16[1,32,768]{2,1,0:T(8,128)(2,1)S(1)} %collective-permute-done) | copy-start | bytes 147460
  13.4 5.5 %collective-permute-start.3 = (bf16[18,1,768]{2,1,0:T(2,128)(2,1)}, bf16[18,1,768]{2,1,0:T(2,128)(2,1)}, u32[]{:S(2)}, u32[]{:S(2)}) collective-permute-start(bf16[18,1,768]{2,1,0:T(2,128)(2,1)} %get-tuple-element.34), channel_id=1, source_target_pairs={{1,0},{2,1},{3,2},{4,3},{5,4},{6,5},{7,6},{8,7},{9,8},{10,9},{11,1... | collective-permute-start | bytes 82952 | tf_op jit(solution)/shard_map/ppermute | solution.py:41
  16.0 9.4 %collective-permute-start.2 = (bf16[18,1,768]{2,1,0:T(2,128)(2,1)}, bf16[18,1,768]{2,1,0:T(2,128)(2,1)}, u32[]{:S(2)}, u32[]{:S(2)}) collective-permute-start(bf16[18,1,768]{2,1,0:T(2,128)(2,1)} %get-tuple-element.35), channel_id=1, source_target_pairs={{0,1},{1,2},{2,3},{3,4},{4,5},{5,6},{6,7},{7,8},{8,9},{9,10},{10,1... | collective-permute-start | bytes 82952 | tf_op jit(solution)/shard_map/ppermute | solution.py:39
  18.6 12.2 %copy-start.15 = (f32[768]{0:T(1024)}, f32[768]{0:T(1024)S(1)}, u32[]{:S(2)}) copy-start(f32[768]{0:T(1024)S(1)} %get-tuple-element.20) | copy-start | bytes 9220
  18.6 12.2 %copy-start.17 = (f32[768]{0:T(1024)}, f32[768]{0:T(1024)S(1)}, u32[]{:S(2)}) copy-start(f32[768]{0:T(1024)S(1)} %get-tuple-element.21) | copy-start | bytes 9220
  31.4 5.6 %copy-start.10 = (f32[8,768]{1,0:T(8,128)}, f32[8,768]{1,0:T(8,128)S(1)}, u32[]{:S(2)}) copy-start(f32[8,768]{1,0:T(8,128)S(1)} %div.38) | copy-start | bytes 73732
  32.2 10.6 %all-to-all-start = ((bf16[16,8,768]{2,1,0:T(8,128)(2,1)}), bf16[16,8,768]{2,1,0:T(8,128)(2,1)}, u32[]{:S(2)}, u32[]{:S(2)}) async-start(bf16[16,8,768]{2,1,0:T(8,128)(2,1)} %broadcast_in_dim.12), calls=%async_computation | async-start | bytes 393216 | tf_op jit(solution)/shard_map/all_to_all | solution.py:50
  64.0 18.8 %all-to-all-start.1 = ((bf16[16,8,1536]{2,1,0:T(8,128)(2,1)}), bf16[16,8,1536]{2,1,0:T(8,128)(2,1)}, u32[]{:S(2)}, u32[]{:S(2)}) async-start(bf16[16,8,1536]{2,1,0:T(8,128)(2,1)} %pad_maximum_fusion.8), calls=%async_computation.1 | async-start | bytes 786432 | tf_op jit(solution)/shard_map/all_to_all | solution.py:130
  73.8 4.0 %copy-start.4 = (bf16[16,32,768]{2,1,0:T(8,128)(2,1)S(1)}, bf16[16,32,768]{2,1,0:T(8,128)(2,1)}, u32[]{:S(2)}) copy-start(bf16[16,32,768]{2,1,0:T(8,128)(2,1)} %param.13) | copy-start | bytes 2359300
  80.0 5.6 %copy-start.11 = (f32[8,768]{1,0:T(8,128)S(1)}, f32[8,768]{1,0:T(8,128)}, u32[]{:S(2)}) copy-start(f32[8,768]{1,0:T(8,128)} %copy-done.10) | copy-start | bytes 73732
  81.2 71.9 %collective-permute-start.8 = (bf16[1536,384]{1,0:T(8,128)(2,1)}, bf16[1536,384]{1,0:T(8,128)(2,1)}, u32[]{:S(2)}, u32[]{:S(2)}) collective-permute-start(bf16[1536,384]{1,0:T(8,128)(2,1)} %pad_maximum_fusion), channel_id=1, source_target_pairs={{0,1},{1,0},{2,3},{3,2},{4,5},{5,4},{6,7},{7,6},{8,9},{9,8},{10,11... | collective-permute-start | bytes 3538952 | tf_op jit(solution)/shard_map/ppermute | solution.py:136
  83.9 3.9 %copy-start.12 = (bf16[8,1536]{1,0:T(8,128)(2,1)}, bf16[8,1536]{1,0:T(8,128)(2,1)S(1)}, u32[]{:S(2)}) copy-start(bf16[8,1536]{1,0:T(8,128)(2,1)S(1)} %reduce_sum.172) | copy-start | bytes 73732
  95.8 93.5 %copy-start.1 = (bf16[16,32,768]{2,1,0:T(8,128)(2,1)}, bf16[16,32,768]{2,1,0:T(8,128)(2,1)S(1)}, u32[]{:S(2)}) copy-start(bf16[16,32,768]{2,1,0:T(8,128)(2,1)S(1)} %get-tuple-element.29) | copy-start | bytes 2359300
  127.2 18.1 %all-to-all-start.3 = ((bf16[128,8,128]{2,1,0:T(8,128)(2,1)}), bf16[128,8,128]{2,1,0:T(8,128)(2,1)}, u32[]{:S(2)}, u32[]{:S(2)}) async-start(bf16[128,8,128]{2,1,0:T(8,128)(2,1)} %bitcast.118), calls=%async_computation.3 | async-start | bytes 524288 | tf_op jit(solution)/shard_map/all_to_all | solution.py:170
  147.2 17.1 %all-to-all-start.4 = ((bf16[8,128,384]{2,1,0:T(8,128)(2,1)}), bf16[8,128,384]{2,1,0:T(8,128)(2,1)}, u32[]{:S(2)}, u32[]{:S(2)}) async-start(bf16[8,128,384]{2,1,0:T(8,128)(2,1)} %broadcast_in_dim.16), calls=%async_computation.4 | async-start | bytes 1572864 | tf_op jit(solution)/shard_map/all_to_all | solution.py:50
  164.2 40.4 %all-to-all-start.2 = ((bf16[64,24,384]{2,1,0:T(8,128)(2,1)}), bf16[64,24,384]{2,1,0:T(8,128)(2,1)}, u32[]{:S(2)}, u32[]{:S(2)}) async-start(bf16[64,24,384]{2,1,0:T(8,128)(2,1)} %bitcast.100), calls=%async_computation.2 | async-start | bytes 2359296 | tf_op jit(solution)/shard_map/all_to_all | solution.py:138
  172.1 17.1 %collective-permute-start.5 = (bf16[1,32,768]{2,1,0:T(8,128)(2,1)S(1)}, bf16[1,32,768]{2,1,0:T(8,128)(2,1)S(1)}, u32[]{:S(2)}, u32[]{:S(2)}) collective-permute-start(bf16[1,32,768]{2,1,0:T(8,128)(2,1)S(1)} %get-tuple-element.37), channel_id=1, source_target_pairs={{16,0},{32,16},{48,32},{64,48},{80,64},{96,80},{112,96},{17,1},{33... | collective-permute-start | bytes 147464 | tf_op jit(solution)/shard_map/ppermute | solution.py:41
  174.9 14.3 %collective-permute-start.4 = (bf16[1,32,768]{2,1,0:T(8,128)(2,1)S(1)}, bf16[1,32,768]{2,1,0:T(8,128)(2,1)S(1)}, u32[]{:S(2)}, u32[]{:S(2)}) collective-permute-start(bf16[1,32,768]{2,1,0:T(8,128)(2,1)S(1)} %get-tuple-element.36), channel_id=1, source_target_pairs={{0,16},{16,32},{32,48},{48,64},{64,80},{80,96},{96,112},{1,17},{17... | collective-permute-start | bytes 147464 | tf_op jit(solution)/shard_map/ppermute | solution.py:39
  189.4 4.4 %collective-permute-start.6 = (bf16[18,1,768]{2,1,0:T(2,128)(2,1)S(1)}, bf16[18,1,768]{2,1,0:T(2,128)(2,1)S(1)}, u32[]{:S(2)}, u32[]{:S(2)}) collective-permute-start(bf16[18,1,768]{2,1,0:T(2,128)(2,1)S(1)} %get-tuple-element.32), channel_id=1, source_target_pairs={{1,0},{2,1},{3,2},{4,3},{5,4},{6,5},{7,6},{8,7},{9,8},{10,9},{11,1... | collective-permute-start | bytes 82952 | tf_op jit(solution)/shard_map/ppermute | solution.py:41
  191.3 9.2 %collective-permute-start.7 = (bf16[18,1,768]{2,1,0:T(2,128)(2,1)S(1)}, bf16[18,1,768]{2,1,0:T(2,128)(2,1)}, u32[]{:S(2)}, u32[]{:S(2)}) collective-permute-start(bf16[18,1,768]{2,1,0:T(2,128)(2,1)S(1)} %get-tuple-element.33), channel_id=1, source_target_pairs={{0,1},{1,2},{2,3},{3,4},{4,5},{5,6},{6,7},{7,8},{8,9},{9,10},{10,1... | collective-permute-start | bytes 82952 | tf_op jit(solution)/shard_map/ppermute | solution.py:39
  202.4 12.2 %copy-start.16 = (f32[768]{0:T(1024)S(1)}, f32[768]{0:T(1024)}, u32[]{:S(2)}) copy-start(f32[768]{0:T(1024)} %copy-done.15) | copy-start | bytes 9220
  202.4 12.2 %copy-start.18 = (f32[768]{0:T(1024)S(1)}, f32[768]{0:T(1024)}, u32[]{:S(2)}) copy-start(f32[768]{0:T(1024)} %copy-done.17) | copy-start | bytes 9220
  202.4 12.2 %copy-start.19 = (f32[768]{0:T(1024)S(1)}, f32[768]{0:T(1024)}, u32[]{:S(2)}) copy-start(f32[768]{0:T(1024)} %get-tuple-element.22) | copy-start | bytes 9220
  202.4 12.2 %copy-start.20 = (f32[768]{0:T(1024)S(1)}, f32[768]{0:T(1024)}, u32[]{:S(2)}) copy-start(f32[768]{0:T(1024)} %get-tuple-element.23) | copy-start | bytes 9220
  202.4 12.2 %copy-start.21 = (f32[768]{0:T(1024)S(1)}, f32[768]{0:T(1024)}, u32[]{:S(2)}) copy-start(f32[768]{0:T(1024)} %get-tuple-element.24) | copy-start | bytes 9220
  202.4 12.2 %copy-start.22 = (f32[768]{0:T(1024)S(1)}, f32[768]{0:T(1024)}, u32[]{:S(2)}) copy-start(f32[768]{0:T(1024)} %get-tuple-element.25) | copy-start | bytes 9220
  202.4 12.2 %copy-start.23 = (f32[768]{0:T(1024)S(1)}, f32[768]{0:T(1024)}, u32[]{:S(2)}) copy-start(f32[768]{0:T(1024)} %get-tuple-element.26) | copy-start | bytes 9220
  207.6 14.7 %all-to-all-start.5 = ((bf16[16,24,384]{2,1,0:T(8,128)(2,1)}), bf16[16,24,384]{2,1,0:T(8,128)(2,1)}, u32[]{:S(2)}, u32[]{:S(2)}) async-start(bf16[16,24,384]{2,1,0:T(8,128)(2,1)} %bitcast.117), calls=%async_computation.5 | async-start | bytes 589824 | tf_op jit(solution)/shard_map/all_to_all | solution.py:179
  (8 other events, 11.1 us)

commit v2 on v1

v2 whole, which is shorter than its diff:
```python
from functools import partial

import jax
import jax.numpy as jnp
from jax import lax
from jax.experimental import pallas as pl
from jax.experimental.pallas import tpu as pltpu
from jax.sharding import PartitionSpec as P

HEADS = 12
HD = 64
POOL = 8
EPSILON = 1e-05
BF = jnp.bfloat16
F32 = jnp.float32
LANES = 128

FINAL = (0, 1, 2, 3, 12, 13, 14, 15)
PARTNER = (5, 4, 7, 6, 9, 8, 11, 10)
SLICE_AT = tuple((FINAL.index(j) if j in FINAL else PARTNER.index(j)) for j in range(16))
PAIRS = [(j, j ^ 1) for j in range(16)]
BOTH = ("row", "col")


def holder(piece, core):
    return FINAL[piece] if FINAL[piece] % 2 == core else PARTNER[piece]


SUM_GROUPS = [[q * 16 + holder(s, c) for s in range(8) for q in range(8)] for c in range(2)]
PLACE_GROUPS = [[q * 16 + holder(s, c) for c in range(2) for q in range(8)] for s in range(8)]


def from_both_sides(first, last, axis):
    count = lax.axis_size(axis)
    before = lax.ppermute(last, axis, [(i, (i + 1) % count) for i in range(count)])
    after = lax.ppermute(first, axis, [((i + 1) % count, i) for i in range(count)])
    return before, after


def edges_of(tile, is_first, is_last):
    top, bottom = from_both_sides(tile[0], tile[-1], "row")
    up = jnp.where(is_first, 0, top).astype(BF)
    down = jnp.where(is_last, 0, bottom).astype(BF)
    first = jnp.concatenate([up[:1], tile[:, 0], down[:1]], axis=0)
    last = jnp.concatenate([up[-1:], tile[:, -1], down[-1:]], axis=0)
    left, right = from_both_sides(first, last, "col")
    return top, bottom, left, right


def copy_for_each(x, axis):
    peers = lax.axis_size(axis)
    return lax.all_to_all(jnp.broadcast_to(x[None], (peers, *x.shape)), axis, 0, 0, tiled=True)


def dot(left, right, dims):
    return lax.dot_general(left, right, ((dims[0], dims[1]), ((), ())), preferred_element_type=F32)


def contract_first(left, right):
    return dot(left, right, ((0,), (0,)))


def contract_last(left, right):
    return dot(left, right, ((1,), (1,)))


def put_sides(padded, flags, top, bottom, left, right):
    padded[0, 8:40, :] = top[...].astype(F32) * flags[0].astype(F32)
    padded[17, 8:40, :] = bottom[...].astype(F32) * flags[1].astype(F32)
    first = left[...].astype(F32) * flags[2].astype(F32)
    last = right[...].astype(F32) * flags[3].astype(F32)
    for row in range(18):
        padded[row, 7:8, :] = first[row : row + 1]
        padded[row, 40:41, :] = last[row : row + 1]


def mix_kernel(
    flags, image, top, bottom, left, right, taps, hidden, standard, inverse, normed, padded, pools
):
    step = pl.program_id(0)
    put_sides(padded, flags, top, bottom, left, right)
    padded[1:17, 8:40, :] = image[...].astype(F32)
    weights = taps[...]
    for cell_row in range(2):
        column = jnp.zeros((32, LANES), F32)
        for row in range(cell_row * POOL, (cell_row + 1) * POOL):
            total = padded[row + 1, 8:40, :]
            for a in range(3):
                for b in range(3):
                    tap = 3 * a + b
                    total = total + weights[tap : tap + 1] * padded[row + a, 7 + b : 39 + b, :]
            rounded = total.astype(BF)
            hidden[row * 32 : (row + 1) * 32, :] = rounded
            column = column + rounded.astype(F32)
        for cell in range(4):
            one = jnp.sum(column[cell * POOL : (cell + 1) * POOL], axis=0, keepdims=True)
            at = 4 * cell_row + cell
            pools[step, at : at + 1, :] = one * (1.0 / (POOL * POOL))

    @pl.when(step == pl.num_programs(0) - 1)
    def _():
        blocks = pools.shape[0]
        scale = 1.0 / (blocks * LANES)
        pooled = [pools[i] for i in range(blocks)]
        centre = sum(jnp.sum(x, axis=1, keepdims=True) for x in pooled) * scale
        moved = [x - centre for x in pooled]
        spread = sum(jnp.sum(x * x, axis=1, keepdims=True) for x in moved) * scale
        factor = lax.rsqrt(spread + EPSILON)
        inverse[...] = jnp.broadcast_to(factor, inverse.shape)
        for i in range(blocks):
            at = slice(i * LANES, (i + 1) * LANES)
            own = moved[i] * factor
            standard[:, at] = own
            normed[:, :, at] = jnp.broadcast_to(own.astype(BF)[None], (16, 8, LANES))


def side_specs():
    return [
        pl.BlockSpec((32, LANES), lambda i: (0, i)),
        pl.BlockSpec((32, LANES), lambda i: (0, i)),
        pl.BlockSpec((18, LANES), lambda i: (0, i)),
        pl.BlockSpec((18, LANES), lambda i: (0, i)),
    ]


SCALARS = pl.BlockSpec(memory_space=pltpu.SMEM)


def mix(flags, image, sides, taps):
    height, width, channels = image.shape
    blocks = channels // LANES
    return pl.pallas_call(
        mix_kernel,
        grid=(blocks,),
        in_specs=[
            SCALARS,
            pl.BlockSpec((height, width, LANES), lambda i: (0, 0, i)),
            *side_specs(),
            pl.BlockSpec((9, LANES), lambda i: (0, i)),
        ],
        out_specs=[
            pl.BlockSpec((height * width, LANES), lambda i: (0, i)),
            pl.BlockSpec((8, channels), lambda i: (0, 0)),
            pl.BlockSpec((8, LANES), lambda i: (0, 0)),
            pl.BlockSpec((16, 8, channels), lambda i: (0, 0, 0)),
        ],
        out_shape=[
            jax.ShapeDtypeStruct((height * width, channels), BF),
            jax.ShapeDtypeStruct((8, channels), F32),
            jax.ShapeDtypeStruct((8, LANES), F32),
            jax.ShapeDtypeStruct((16, 8, channels), BF),
        ],
        scratch_shapes=[pltpu.VMEM((18, 48, LANES), F32), pltpu.VMEM((blocks, 8, LANES), F32)],
        cost_estimate=pl.CostEstimate(flops=8_000_000, bytes_accessed=2_000_000, transcendentals=0),
        name="mix",
    )(flags, image, *sides, taps)


def attend_kernel(query, dout, cells, w_key, w_value, attended, grad_query, sums):
    low = lax.broadcasted_iota(jnp.int32, (128, LANES), 1) < HD
    all_cells = cells[...]
    zero = jnp.zeros((128, LANES), BF)

    def two_heads(weight):
        both = jnp.dot(all_cells, weight[...], preferred_element_type=F32).astype(BF)
        return jnp.concatenate([jnp.where(low, both, zero), jnp.where(low, zero, both)], axis=0)

    keys = two_heads(w_key) * jnp.asarray(HD**-0.5, BF)
    values = two_heads(w_value)
    q, d = query[...], dout[...]
    grads = contract_last(d, values)
    expons = jnp.exp(contract_last(q, keys))
    probs, scores = [], []
    for head in range(2):
        own = expons[:, head * 128 : (head + 1) * 128]
        prob = own / jnp.sum(own, axis=1, keepdims=True)
        grad = grads[:, head * 128 : (head + 1) * 128]
        delta = jnp.sum(prob * grad, axis=1, keepdims=True)
        probs.append(prob.astype(BF))
        scores.append((prob * (grad - delta)).astype(BF))
    weights = jnp.concatenate(probs, axis=1)
    grad_scores = jnp.concatenate(scores, axis=1)
    attended[...] = jnp.dot(weights, values, preferred_element_type=F32).astype(BF)
    grad_query[...] = jnp.dot(grad_scores, keys, preferred_element_type=F32).astype(BF)
    grad_keys = contract_first(grad_scores, q)
    grad_values = contract_first(weights, d)
    grad_keys = jnp.where(low, grad_keys[:128], grad_keys[128:]) * (HD**-0.5)
    grad_values = jnp.where(low, grad_values[:128], grad_values[128:])
    sums[:, 0] = grad_keys.astype(BF).reshape(16, 8, LANES)
    sums[:, 1] = grad_values.astype(BF).reshape(16, 8, LANES)


def attend(query, dout, cells, w_key, w_value):
    tokens, channels = query.shape
    blocks = channels // LANES
    by_pair = pl.BlockSpec((tokens, LANES), lambda i: (0, i))
    weight = pl.BlockSpec((channels, LANES), lambda i: (0, i))
    return pl.pallas_call(
        attend_kernel,
        grid=(blocks,),
        in_specs=[
            by_pair,
            by_pair,
            pl.BlockSpec((128, channels), lambda i: (0, 0)),
            weight,
            weight,
        ],
        out_specs=[by_pair, by_pair, pl.BlockSpec((16, 2, 8, LANES), lambda i: (0, 0, 0, i))],
        out_shape=[
            jax.ShapeDtypeStruct((tokens, channels), BF),
            jax.ShapeDtypeStruct((tokens, channels), BF),
            jax.ShapeDtypeStruct((16, 2, 8, channels), BF),
        ],
        cost_estimate=pl.CostEstimate(
            flops=3_000_000_000, bytes_accessed=6_000_000, transcendentals=800_000
        ),
        name="attend",
    )(query, dout, cells, w_key, w_value)


def taps_kernel(flags, image, top, bottom, left, right, early, terms, windows, padded, lines):
    put_sides(padded, flags, top, bottom, left, right)
    padded[1:17, 8:40, :] = image[...].astype(F32)
    totals = [jnp.zeros((8, LANES), F32) for _ in range(9)]
    for row in range(16):
        grad = early[row]
        for a in range(3):
            for b in range(3):
                part = grad * padded[row + a, 7 + b : 39 + b, :]
                totals[3 * a + b] = totals[3 * a + b] + (
                    (part[:8] + part[8:16]) + (part[16:24] + part[24:])
                )
    for tap in range(9):
        terms[tap : tap + 1, :] = jnp.sum(totals[tap], axis=0, keepdims=True)
    for cell_row in range(2):
        for a in range(3):
            at = cell_row * POOL + a
            line = padded[at]
            for row in range(at + 1, at + POOL):
                line = line + padded[row]
            lines[...] = line
            for b in range(3):
                for cell in range(4):
                    part = lines[7 + b + 8 * cell : 15 + b + 8 * cell, :]
                    place = 4 * cell_row + cell
                    windows[3 * a + b, place : place + 1, :] = jnp.sum(part, axis=0, keepdims=True)


def tap_terms(flags, image, sides, early):
    height, width, channels = image.shape
    block = pl.BlockSpec((height, width, LANES), lambda i: (0, 0, i))
    return pl.pallas_call(
        taps_kernel,
        grid=(channels // LANES,),
        in_specs=[SCALARS, block, *side_specs(), block],
        out_specs=[
            pl.BlockSpec((9, LANES), lambda i: (0, i)),
            pl.BlockSpec((9, 8, LANES), lambda i: (0, 0, i)),
        ],
        out_shape=[
            jax.ShapeDtypeStruct((9, channels), F32),
            jax.ShapeDtypeStruct((9, 8, channels), F32),
        ],
        scratch_shapes=[pltpu.VMEM((18, 48, LANES), F32), pltpu.VMEM((48, LANES), F32)],
        cost_estimate=pl.CostEstimate(flops=8_000_000, bytes_accessed=3_000_000, transcendentals=0),
        name="tap_terms",
    )(flags, image, *sides, early)


def window_of(x, start):
    base = min(start // LANES * LANES, x.shape[1] - 2 * LANES)
    if start == base:
        return x[:, base : base + LANES]
    return pltpu.roll(x[:, base : base + 2 * LANES], base - start + 2 * LANES, 1)[:, :LANES]


def cells_kernel(terms, w_key, w_value, standard, inverse, early, windows, grad_pooled, blocks):
    received = jnp.sum(terms[...].astype(F32), axis=0)
    keys, values = received[0], received[1]
    grad = contract_last(keys.astype(BF), w_key[...]) + contract_last(values.astype(BF), w_value[...])
    own = standard[...]
    scale = 1.0 / own.shape[1]
    centre = jnp.sum(grad, axis=1, keepdims=True) * scale
    along = jnp.sum(grad * own, axis=1, keepdims=True) * scale
    pooled = (grad - centre - own * along) * (inverse[:, :1] * (1.0 / (POOL * POOL)))
    grad_pooled[...] = pooled
    conv = [
        early[t : t + 1, :] + jnp.sum(pooled * windows[t], axis=0, keepdims=True) for t in range(9)
    ]
    first, last = jnp.concatenate(conv[:8], axis=0), jnp.broadcast_to(conv[8], (8, own.shape[1]))
    lane = lax.broadcasted_iota(jnp.int32, (8, LANES), 1)
    both = jnp.concatenate([keys, values], axis=1)
    width = own.shape[1] // 16
    pieces = {}
    for j in range(16):
        part = PARTNER[SLICE_AT[j]] - 4
        taps = pltpu.roll(window_of(first, width * j), 24, 1)
        tail = pltpu.roll(window_of(last, width * j), 72, 1)
        rest = jnp.where(lane < 72, taps, tail)
        for q in range(8):
            if (part, q) not in pieces:
                pieces[part, q] = window_of(both, 192 * part + 24 * q)
            blocks[16 * q + j] = jnp.where(lane < 24, pieces[part, q], rest).astype(BF)


def at_cells(terms, w_key, w_value, standard, inverse, early, windows):
    channels = standard.shape[1]
    return pl.pallas_call(
        cells_kernel,
        out_shape=[
            jax.ShapeDtypeStruct((8, channels), F32),
            jax.ShapeDtypeStruct((128, 8, LANES), BF),
        ],
        cost_estimate=pl.CostEstimate(flops=30_000_000, bytes_accessed=3_500_000, transcendentals=0),
        name="at_cells",
    )(terms, w_key, w_value, standard, inverse, early, windows)


def pieces_kernel(flags, got, blocks, cells, placed, conv):
    piece = jnp.sum(got[...].astype(F32), axis=0).astype(BF)
    received = blocks[...]
    conv[...] = jnp.sum(received.astype(F32), axis=0)
    cell_piece = contract_first(received.reshape(1024, LANES), cells[...])[:24].astype(BF)
    odd = flags[4] == 1
    first = jnp.where(odd, cell_piece, piece)
    second = jnp.where(odd, piece, cell_piece)
    for q in range(8):
        placed[q] = first
        placed[8 + q] = second


def pieces(flags, got, blocks, cells):
    half = cells.shape[1]
    vmem = pl.BlockSpec(memory_space=pltpu.VMEM)
    return pl.pallas_call(
        pieces_kernel,
        in_specs=[SCALARS, vmem, vmem, vmem],
        out_shape=[
            jax.ShapeDtypeStruct((16, 24, half), BF),
            jax.ShapeDtypeStruct((8, LANES), F32),
        ],
        cost_estimate=pl.CostEstimate(flops=100_000_000, bytes_accessed=2_500_000, transcendentals=0),
        name="pieces",
    )(flags, got, blocks, cells)


def unmix_kernel(flags, early, pooled, top, bottom, left, right, taps, image, padded):
    put_sides(padded, flags, top, bottom, left, right)
    for row in range(16):
        for cell in range(4):
            place = 4 * (row // POOL) + cell
            at = slice(8 * cell, 8 * cell + 8)
            padded[row + 1, 8 + 8 * cell : 16 + 8 * cell, :] = (
                early[row, at, :] + pooled[place : place + 1, :]
            )
    weights = taps[...]
    for row in range(16):
        total = padded[row + 1, 8:40, :]
        for a in range(3):
            for b in range(3):
                tap = 3 * a + b
                total = total + weights[tap : tap + 1] * padded[row + 2 - a, 9 - b : 41 - b, :]
        image[row] = total.astype(BF)


def unmix(flags, early, pooled, sides, taps):
    height, width, channels = early.shape
    block = pl.BlockSpec((height, width, LANES), lambda i: (0, 0, i))
    return pl.pallas_call(
        unmix_kernel,
        grid=(channels // LANES,),
        in_specs=[
            SCALARS,
            block,
            pl.BlockSpec((8, LANES), lambda i: (0, i)),
            *side_specs(),
            pl.BlockSpec((9, LANES), lambda i: (0, i)),
        ],
        out_specs=block,
        out_shape=jax.ShapeDtypeStruct((height, width, channels), BF),
        scratch_shapes=[pltpu.VMEM((18, 48, LANES), F32)],
        cost_estimate=pl.CostEstimate(flops=8_000_000, bytes_accessed=3_000_000, transcendentals=0),
        name="unmix",
    )(flags, early, pooled, *sides, taps)


def on_device(image, conv_taps, w_query, w_key, w_value, w_out, grad_out):
    height, width, channels = image.shape
    half = channels // 2
    at_row, at_col = lax.axis_index("row"), lax.axis_index("col")
    core = at_col % 2
    is_first, is_last = at_row == 0, at_row == lax.axis_size("row") - 1
    turned = (core == 1) ^ ((at_col >= 4) & (at_col < 12))
    flags = jnp.stack(
        [
            ~is_first,
            ~is_last,
            at_col > 0,
            at_col < lax.axis_size("col") - 1,
            turned,
        ]
    ).astype(jnp.int32)
    flat_grad = grad_out.reshape(-1, channels)
    sides = edges_of(image, is_first, is_last)
    dout = contract_last(flat_grad, w_out).astype(BF)
    hidden, standard, inverse, normed = mix(flags, image, sides, conv_taps)
    cells = lax.all_to_all(normed, "col", 0, 0, tiled=True).reshape(-1, channels)
    query = jnp.dot(hidden, w_query, preferred_element_type=F32).astype(BF)
    cells_half = lax.dynamic_slice_in_dim(cells, core * half, half, axis=1)
    all_cells = copy_for_each(cells_half, "row").reshape(-1, half)
    attended, grad_query, sums = attend(query, dout, cells, w_key, w_value)
    terms = lax.all_to_all(sums, "col", 0, 0, tiled=True)

    def half_terms(which):
        h = lax.dynamic_slice_in_dim(hidden, which * half, half, axis=1)
        a = lax.dynamic_slice_in_dim(attended, which * half, half, axis=1)
        return jnp.concatenate([contract_first(grad_query, h), contract_first(flat_grad, a)], axis=0)

    theirs = lax.ppermute(half_terms(1 - core).astype(BF), "col", PAIRS)
    chip = (half_terms(core) + theirs.astype(F32)).astype(BF)
    got = lax.all_to_all(
        chip.reshape(64, 24, half), BOTH, 0, 0, tiled=True, axis_index_groups=SUM_GROUPS
    )
    grad_hidden = contract_last(grad_query, w_query)
    early = (flat_grad.astype(F32) + grad_hidden).reshape(height, width, channels)
    early_terms, windows = tap_terms(flags, image, sides, early)
    pooled, block = at_cells(terms, w_key, w_value, standard, inverse, early_terms, windows)
    blocks = lax.all_to_all(block, BOTH, 0, 0, tiled=True)
    rows = jnp.repeat(pooled, POOL, axis=0).reshape(2, width, channels)
    up = jnp.concatenate([pooled[0:1], pooled[4:5]], axis=0)
    down = jnp.concatenate([pooled[3:4], pooled[7:8]], axis=0)
    top, bottom = from_both_sides(
        (early[0] + rows[0]).astype(BF), (early[-1] + rows[1]).astype(BF), "row"
    )
    first = (early[:, 0] + jnp.repeat(up, POOL, axis=0)).astype(BF)
    last = (early[:, -1] + jnp.repeat(down, POOL, axis=0)).astype(BF)
    over = jnp.where(is_first, 0, top).astype(BF)
    under = jnp.where(is_last, 0, bottom).astype(BF)
    left, right = from_both_sides(
        jnp.concatenate([over[:1], first, under[:1]], axis=0),
        jnp.concatenate([over[-1:], last, under[-1:]], axis=0),
        "col",
    )
    grad_image = unmix(flags, early, pooled, (top, bottom, left, right), conv_taps)
    placed, conv = pieces(flags, got, blocks, all_cells)
    placed = lax.all_to_all(
        placed, BOTH, 0, 0, tiled=True, axis_index_groups=PLACE_GROUPS
    )
    grad_weights = jnp.transpose(placed.reshape(2, 192, half), (0, 2, 1)).reshape(channels, 192)
    grad_conv = jnp.concatenate([conv[:, 24:72], conv[:1, 72:120]], axis=0)
    return (grad_image, grad_weights.astype(F32), grad_conv)


def solution(mesh):
    return jax.shard_map(
        on_device,
        mesh=mesh,
        in_specs=(P("row", "col", None), P(), P(), P(), P(), P(), P("row", "col", None)),
        out_specs=(P("row", "col", None), P(None, "col"), P(None, "col")),
        check_vma=False,
    )
```

time: 228 us -> 165 us (0.72)
  the two profiles are of different devices: /device:TPU:96 before, /device:TPU:0 now
where the time goes in v2:
time: 165 us; the launch traced here: 163 us
  waiting for transfers between devices  50.5 us (31%)
  starting transfers between devices  48.6 us (29%)
  Pallas kernels  30.6 us (19%)
  matrix products  12.6 us (8%)
  local copies, waits for them, and re-layouts  12.2 us (7%)
  other arithmetic  7.5 us (5%)
    all_to_all x1, waiting for transfers between devices, on_device(): lax.all_to_all(chip.reshape(64, 24, half), BOTH, 0, 0, tiled=True, axis_i...  18 us
    ppermute x4, starting transfers between devices, from_both_sides(): lax.ppermute(first, axis, [((i + 1) % count, i) for i in range(count)])  13.5 us
    dot_general x6, matrix products, dot(): lax.dot_general(left, right, ((dims[0], dims[1]), ((), ())), preferred_el...  9.8 us
    ppermute x4, waiting for transfers between devices, from_both_sides(): lax.ppermute(last, axis, [(i, (i + 1) % count) for i in range(count)])  9.4 us
    pallas_call x1, Pallas kernels, attend(): pl.pallas_call(attend_kernel, grid=(blocks,), in_specs=[by_pair, by_pair,...  8.61 us
    all_to_all x1, starting transfers between devices, on_device(): blocks = lax.all_to_all(block, BOTH, 0, 0, tiled=True)  8.41 us
    all_to_all x1, waiting for transfers between devices, on_device(): blocks = lax.all_to_all(block, BOTH, 0, 0, tiled=True)  7.79 us
    all_to_all x1, starting transfers between devices, on_device(): lax.all_to_all(chip.reshape(64, 24, half), BOTH, 0, 0, tiled=True, axis_i...  6.24 us
  transfers between devices with their start and end apart: 15, of which 10 were waited for; matrix products, arithmetic and copies ran while one was open for 13% of the time, Pallas kernels for 9%

profile of v2, /device:TPU:0, one launch (start us, length us, event | category | flops | bytes accessed | tf_op | source)
XLA Modules:
  0.0 162.9 jit_solution(16480803834487308767)
XLA Ops:
  1.6 2.1 %collective-permute-start = (bf16[32,768]{1,0:T(8,128)(2,1)S(1)}, bf16[32,768]{1,0:T(8,128)(2,1)S(1)}, u32[]{:S(2)}, u32[]{:S(2)}) collective-permute-start(bf16[32,768]{1,0:T(8,128)(2,1)S(1)} %get-tuple-element.36), channel_id=1, source_target_pairs={{0,16},{16,32},{32,48},{48,64},{64,80},{80,96},{96,112},{112,0},{1... | collective-permute-start | bytes 147464 | tf_op jit(solution)/shard_map/ppermute | solution.py:35
  3.7 2.3 %collective-permute-start.1 = (bf16[32,768]{1,0:T(8,128)(2,1)S(1)}, bf16[32,768]{1,0:T(8,128)(2,1)S(1)}, u32[]{:S(2)}, u32[]{:S(2)}) collective-permute-start(bf16[32,768]{1,0:T(8,128)(2,1)S(1)} %get-tuple-element.35), channel_id=1, source_target_pairs={{16,0},{32,16},{48,32},{64,48},{80,64},{96,80},{112,96},{0,112},{1... | collective-permute-start | bytes 147464 | tf_op jit(solution)/shard_map/ppermute | solution.py:36
  8.3 4.4 %collective-permute-start.3 = (bf16[18,768]{1,0:T(8,128)(2,1)S(1)}, bf16[18,768]{1,0:T(8,128)(2,1)S(1)}, u32[]{:S(2)}, u32[]{:S(2)}) collective-permute-start(bf16[18,768]{1,0:T(8,128)(2,1)S(1)} %pad_maximum_fusion.2), channel_id=1, source_target_pairs={{1,0},{2,1},{3,2},{4,3},{5,4},{6,5},{7,6},{8,7},{9,8},{10,9},{11,1... | collective-permute-start | bytes 82952 | tf_op jit(solution)/shard_map/ppermute | solution.py:36
  12.8 3.2 %convolution_convert_fusion.dout = bf16[512,768]{1,0:T(8,128)(2,1)} fusion(bf16[512,768]{1,0:T(8,128)(2,1)} %bitcast.66, bf16[768,768]{1,0:T(8,128)(2,1)} %param.12), kind=kOutput, calls=%fused_computation.4 | convolution fusion | flops 604372992 | bytes 2752512 | tf_op jit(solution)/shard_map/dot_general | solution.py:56
  16.8 3.1 %collective-permute-done.2.left = bf16[18,768]{1,0:T(8,128)(2,1)S(1)} collective-permute-done((bf16[18,768]{1,0:T(8,128)(2,1)S(1)}, bf16[18,768]{1,0:T(8,128)(2,1)S(1)}, u32[]{:S(2)}, u32[]{:S(2)}) %collective-permute-start.2) | collective-permute-done | bytes 27680 | tf_op jit(solution)/shard_map/ppermute | solution.py:35
  20.4 5.2 %mix.1 = (bf16[512,768]{1,0:T(8,128)(2,1)}, f32[8,768]{1,0:T(8,128)}, f32[8,128]{1,0:T(8,128)}, bf16[16,8,768]{2,1,0:T(8,128)(2,1)}) custom-call(s32[5]{0:T(128)} %convert_element_type.48.flags, bf16[16,32,768]{2,1,0:T(8,128)(2,1)} %image.3, bf16[32,768]{1,0:T(8,128)(2,1)} %copy-done.7, bf16[32,768]{1,0:T(8,128)(2,1)} %copy-done.8, ...), custom_call_target="tpu_custom_call" | custom-call | flops 8000000 | bytes 2000000 | tf_op jit(solution)/shard_map/mix/pallas_call | solution.py:132
  25.6 4.3 %all-to-all-start = ((bf16[16,8,768]{2,1,0:T(8,128)(2,1)}), bf16[16,8,768]{2,1,0:T(8,128)(2,1)S(1)}, u32[]{:S(2)}, u32[]{:S(2)}) async-start(bf16[16,8,768]{2,1,0:T(8,128)(2,1)} %get-tuple-element.17), calls=%async_computation | async-start | bytes 393216 | tf_op jit(solution)/shard_map/all_to_all | solution.py:407
  29.9 2.8 %convolution_convert_fusion.1.query = bf16[512,768]{1,0:T(8,128)(2,1)} fusion(bf16[512,768]{1,0:T(8,128)(2,1)} %get-tuple-element.16, bf16[768,768]{1,0:T(8,128)(2,1)S(1)} %copy-done), kind=kOutput, calls=%fused_computation.5 | convolution fusion | flops 604372992 | bytes 2752512 | tf_op jit(solution)/shard_map/dot_general | solution.py:408
  32.7 5.7 %all-to-all-done = bf16[16,8,768]{2,1,0:T(8,128)(2,1)S(1)} async-done(((bf16[16,8,768]{2,1,0:T(8,128)(2,1)}), bf16[16,8,768]{2,1,0:T(8,128)(2,1)S(1)}, u32[]{:S(2)}, u32[]{:S(2)}) %all-to-all-start) | async-done | bytes 196640 | tf_op jit(solution)/shard_map/all_to_all | solution.py:407
  39.2 8.6 %attend.1 = (bf16[512,768]{1,0:T(8,128)(2,1)}, bf16[512,768]{1,0:T(8,128)(2,1)}, bf16[16,2,8,768]{3,2,1,0:T(8,128)(2,1)}) custom-call(bf16[512,768]{1,0:T(8,128)(2,1)} %convolution_convert_fusion.1.query, bf16[512,768]{1,0:T(8,128)(2,1)} %convolution_convert_fusion.dout, bf16[128,768]{1,0:T(8,128)(2,1)} %bitcast.72, bf16[768,768]{1,0:T(8,128)(2,1)} %w_key.3, ...), custom_call_target="tpu_custom_call" | custom-call | flops 3000000000 | bytes 6000000 | tf_op jit(solution)/shard_map/attend/pallas_call | solution.py:198
  47.8 2.1 %convert_add_fusion = f32[512,768]{1,0:T(8,128)S(1)} fusion(bf16[512,768]{1,0:T(8,128)(2,1)S(1)} %bitcast.67, bf16[512,768]{1,0:T(8,128)(2,1)} %get-tuple-element.18, bf16[768,768]{1,0:T(8,128)(2,1)S(1)} %copy-done), kind=kOutput, calls=%fused_computation.2 | convolution fusion | flops 604766208 | bytes 4325376 | tf_op jit(solution)/shard_map/dot_general | solution.py:56
  53.4 1.7 %fusion.5 = f32[768,384]{1,0:T(8,128)} fusion(bf16[512,768]{1,0:T(8,128)(2,1)S(1)} %copy-done.5, bf16[512,768]{1,0:T(8,128)(2,1)S(1)} %copy-done.11, s32[]{:T(128)S(6)} %select_n.45), kind=kOutput, calls=%fused_computation.14 | convolution fusion | flops 301989888 | bytes 2359300 | tf_op jit(solution)/shard_map/dot_general | solution.py:56
  55.1 4.2 %all-to-all-start.1 = ((bf16[16,2,8,768]{3,2,1,0:T(8,128)(2,1)}), bf16[16,2,8,768]{3,2,1,0:T(8,128)(2,1)}, u32[]{:S(2)}, u32[]{:S(2)}) async-start(bf16[16,2,8,768]{3,2,1,0:T(8,128)(2,1)} %get-tuple-element.19), calls=%async_computation.1 | async-start | bytes 786432 | tf_op jit(solution)/shard_map/all_to_all | solution.py:412
  60.0 5.5 %tap_terms.1 = (f32[9,768]{1,0:T(8,128)}, f32[9,8,768]{2,1,0:T(8,128)}) custom-call(s32[5]{0:T(128)} %convert_element_type.48.flags, bf16[16,32,768]{2,1,0:T(8,128)(2,1)} %image.3, bf16[32,768]{1,0:T(8,128)(2,1)} %copy-done.7, bf16[32,768]{1,0:T(8,128)(2,1)} %copy-done.8, bf16[18,768]{1,0:T(8,128)(2,1)} %copy-done.15, bf16[18,768]{1,0:T(8,128)(2,1)} %copy-done.14, ...), custom_call_target="tpu_custom_call" | custom-call | flops 8000000 | bytes 3000000 | tf_op jit(solution)/shard_map/tap_terms/pallas_call | solution.py:252
  66.2 1.6 convolution_bitcast_fusion
  67.8 2.2 %all-to-all-done.1.terms = bf16[16,2,8,768]{3,2,1,0:T(8,128)(2,1)} async-done(((bf16[16,2,8,768]{3,2,1,0:T(8,128)(2,1)}), bf16[16,2,8,768]{3,2,1,0:T(8,128)(2,1)}, u32[]{:S(2)}, u32[]{:S(2)}) %all-to-all-start.1) | async-done | bytes 393248 | tf_op jit(solution)/shard_map/all_to_all | solution.py:412
  70.0 3.6 %at_cells.1 = (f32[8,768]{1,0:T(8,128)}, bf16[128,8,128]{2,1,0:T(8,128)(2,1)}) custom-call(bf16[16,2,8,768]{3,2,1,0:T(8,128)(2,1)} %all-to-all-done.1.terms, bf16[768,768]{1,0:T(8,128)(2,1)} %w_key.3, bf16[768,768]{1,0:T(8,128)(2,1)} %w_value.3, f32[8,768]{1,0:T(8,128)} %get-tuple-element.20.standard, f32[8,128]{1,0:T(8,128)} %get-tuple-element.21.inverse, ...), custom_call_target="tpu_custom_call" | custom-call | flops 30000000 | bytes 3500000 | tf_op jit(solution)/shard_map/at_cells/pallas_call | solution.py:308
  73.5 8.4 %all-to-all-start.3 = ((bf16[128,8,128]{2,1,0:T(8,128)(2,1)}), bf16[128,8,128]{2,1,0:T(8,128)(2,1)}, u32[]{:S(2)}, u32[]{:S(2)}) async-start(bf16[128,8,128]{2,1,0:T(8,128)(2,1)} %get-tuple-element.26), calls=%async_computation.3 | async-start | bytes 524288 | tf_op jit(solution)/shard_map/all_to_all | solution.py:428
  84.4 7.8 %all-to-all-done.3.blocks = bf16[128,8,128]{2,1,0:T(8,128)(2,1)} async-done(((bf16[128,8,128]{2,1,0:T(8,128)(2,1)}), bf16[128,8,128]{2,1,0:T(8,128)(2,1)}, u32[]{:S(2)}, u32[]{:S(2)}) %all-to-all-start.3) | async-done | bytes 262176 | tf_op jit(solution)/shard_map/all_to_all | solution.py:428
  92.2 1.8 %broadcast_in_dim.29 = bf16[8,128,384]{2,1,0:T(8,128)(2,1)} broadcast(bf16[128,384]{1,0:T(8,128)(2,1)} %constant_dynamic-slice_fusion), dimensions={1,2} | broadcast | bytes 884736 | tf_op jit(solution)/shard_map/broadcast_in_dim | solution.py:52
  94.0 4.2 %all-to-all-start.4 = ((bf16[8,128,384]{2,1,0:T(8,128)(2,1)}), bf16[8,128,384]{2,1,0:T(8,128)(2,1)}, u32[]{:S(2)}, u32[]{:S(2)}) async-start(bf16[8,128,384]{2,1,0:T(8,128)(2,1)} %broadcast_in_dim.29), calls=%async_computation.4 | async-start | bytes 1572864 | tf_op jit(solution)/shard_map/all_to_all | solution.py:52
  99.1 2.0 %collective-permute-start.4 = (bf16[32,768]{1,0:T(8,128)(2,1)}, bf16[32,768]{1,0:T(8,128)(2,1)}, u32[]{:S(2)}, u32[]{:S(2)}) collective-permute-start(bf16[32,768]{1,0:T(8,128)(2,1)} %get-tuple-element.32), channel_id=1, source_target_pairs={{0,16},{16,32},{32,48},{48,64},{64,80},{80,96},{96,112},{112,0},{1... | collective-permute-start | bytes 147464 | tf_op jit(solution)/shard_map/ppermute | solution.py:35
  101.1 2.2 %collective-permute-start.5 = (bf16[32,768]{1,0:T(8,128)(2,1)}, bf16[32,768]{1,0:T(8,128)(2,1)}, u32[]{:S(2)}, u32[]{:S(2)}) collective-permute-start(bf16[32,768]{1,0:T(8,128)(2,1)} %get-tuple-element.31), channel_id=1, source_target_pairs={{16,0},{32,16},{48,32},{64,48},{80,64},{96,80},{112,96},{0,112},{1... | collective-permute-start | bytes 147464 | tf_op jit(solution)/shard_map/ppermute | solution.py:36
  103.4 2.6 %fusion = bf16[1536,384]{1,0:T(8,128)(2,1)} fusion(f32[768,384]{1,0:T(8,128)S(1)} %convolution_bitcast_fusion, f32[768,384]{1,0:T(8,128)S(1)} %copy-done.3, bf16[1536,384]{1,0:T(8,128)(2,1)} %collective-permute-done.8), kind=kLoop, calls=%fused_computation.1 | loop fusion | flops 2359296 | bytes 4718592 | tf_op jit(solution)/shard_map/convert_element_type | solution.py:420
  105.9 5.5 %all-to-all-done.4 = bf16[8,128,384]{2,1,0:T(8,128)(2,1)} async-done(((bf16[8,128,384]{2,1,0:T(8,128)(2,1)}), bf16[8,128,384]{2,1,0:T(8,128)(2,1)}, u32[]{:S(2)}, u32[]{:S(2)}) %all-to-all-start.4) | async-done | bytes 786464 | tf_op jit(solution)/shard_map/all_to_all | solution.py:52
  111.4 6.2 %all-to-all-start.2 = ((bf16[64,24,384]{2,1,0:T(8,128)(2,1)}), bf16[64,24,384]{2,1,0:T(8,128)(2,1)S(1)}, u32[]{:S(2)}, u32[]{:S(2)}) async-start(bf16[64,24,384]{2,1,0:T(8,128)(2,1)} %bitcast.65), calls=%async_computation.2 | async-start | bytes 2359296 | tf_op jit(solution)/shard_map/all_to_all | solution.py:421
  118.6 18.0 %all-to-all-done.2.got = bf16[64,24,384]{2,1,0:T(8,128)(2,1)S(1)} async-done(((bf16[64,24,384]{2,1,0:T(8,128)(2,1)}), bf16[64,24,384]{2,1,0:T(8,128)(2,1)S(1)}, u32[]{:S(2)}, u32[]{:S(2)}) %all-to-all-start.2) | async-done | bytes 1179680 | tf_op jit(solution)/shard_map/all_to_all | solution.py:421
  137.7 2.7 %pieces.1 = (bf16[16,24,384]{2,1,0:T(8,128)(2,1)}, f32[8,128]{1,0:T(8,128)}) custom-call(s32[5]{0:T(128)} %convert_element_type.48.flags, bf16[64,24,384]{2,1,0:T(8,128)(2,1)} %copy-done.2, bf16[128,8,128]{2,1,0:T(8,128)(2,1)} %all-to-all-done.3.blocks, bf16[1024,384]{1,0:T(8,128)(2,1)} %bitcast.21.cells), custom_call_target="tpu_custom_call" | custom-call | flops 100000000 | bytes 2500000 | tf_op jit(solution)/shard_map/pieces/pallas_call | solution.py:335
  140.4 3.5 %all-to-all-start.5 = ((bf16[16,24,384]{2,1,0:T(8,128)(2,1)}), bf16[16,24,384]{2,1,0:T(8,128)(2,1)S(1)}, u32[]{:S(2)}, u32[]{:S(2)}) async-start(bf16[16,24,384]{2,1,0:T(8,128)(2,1)} %get-tuple-element.27), calls=%async_computation.5 | async-start | bytes 589824 | tf_op jit(solution)/shard_map/all_to_all | solution.py:446
  144.0 4.6 %collective-permute-start.7 = (bf16[18,768]{1,0:T(8,128)(2,1)S(1)}, bf16[18,768]{1,0:T(8,128)(2,1)S(1)}, u32[]{:S(2)}, u32[]{:S(2)}) collective-permute-start(bf16[18,768]{1,0:T(8,128)(2,1)S(1)} %pad_maximum_fusion.4), channel_id=1, source_target_pairs={{1,0},{2,1},{3,2},{4,3},{5,4},{6,5},{7,6},{8,7},{9,8},{10,9},{11,1... | collective-permute-start | bytes 82952 | tf_op jit(solution)/shard_map/ppermute | solution.py:36
  150.3 5.4 %collective-permute-done.6.left = bf16[18,768]{1,0:T(8,128)(2,1)S(1)} collective-permute-done((bf16[18,768]{1,0:T(8,128)(2,1)S(1)}, bf16[18,768]{1,0:T(8,128)(2,1)S(1)}, u32[]{:S(2)}, u32[]{:S(2)}) %collective-permute-start.6) | collective-permute-done | bytes 27680 | tf_op jit(solution)/shard_map/ppermute | solution.py:35
  156.3 5.0 %unmix.1 = bf16[16,32,768]{2,1,0:T(8,128)(2,1)} custom-call(s32[5]{0:T(128)} %convert_element_type.48.flags, f32[16,32,768]{2,1,0:T(8,128)} %bitcast.64, f32[8,768]{1,0:T(8,128)} %get-tuple-element.24.pooled, bf16[32,768]{1,0:T(8,128)(2,1)} %collective-permute-done.4.top, bf16[32,768]{1,0:T(8,128)(2,1)} %collective-permute-done.5.bottom, ...), custom_call_target="tpu_custom_call" | custom-call | flops 8000000 | bytes 3000000 | tf_op jit(solution)/shard_map/unmix/pallas_call | solution.py:369
  (83 shorter events, 19.5 us)
Async XLA Ops:
  0.6 29.3 %copy-start = (bf16[768,768]{1,0:T(8,128)(2,1)S(1)}, bf16[768,768]{1,0:T(8,128)(2,1)}, u32[]{:S(2)}) copy-start(bf16[768,768]{1,0:T(8,128)(2,1)} %param.9) | copy-start | bytes 3538948
  1.6 6.4 %collective-permute-start = (bf16[32,768]{1,0:T(8,128)(2,1)S(1)}, bf16[32,768]{1,0:T(8,128)(2,1)S(1)}, u32[]{:S(2)}, u32[]{:S(2)}) collective-permute-start(bf16[32,768]{1,0:T(8,128)(2,1)S(1)} %get-tuple-element.36), channel_id=1, source_target_pairs={{0,16},{16,32},{32,48},{48,64},{64,80},{80,96},{96,112},{112,0},{1... | collective-permute-start | bytes 147464 | tf_op jit(solution)/shard_map/ppermute | solution.py:35
  3.7 4.6 %collective-permute-start.1 = (bf16[32,768]{1,0:T(8,128)(2,1)S(1)}, bf16[32,768]{1,0:T(8,128)(2,1)S(1)}, u32[]{:S(2)}, u32[]{:S(2)}) collective-permute-start(bf16[32,768]{1,0:T(8,128)(2,1)S(1)} %get-tuple-element.35), channel_id=1, source_target_pairs={{16,0},{32,16},{48,32},{64,48},{80,64},{96,80},{112,96},{0,112},{1... | collective-permute-start | bytes 147464 | tf_op jit(solution)/shard_map/ppermute | solution.py:36
  8.0 8.1 %copy-start.7 = (bf16[32,768]{1,0:T(8,128)(2,1)}, bf16[32,768]{1,0:T(8,128)(2,1)S(1)}, u32[]{:S(2)}) copy-start(bf16[32,768]{1,0:T(8,128)(2,1)S(1)} %collective-permute-done.top) | copy-start | bytes 147460
  8.3 7.8 %copy-start.8 = (bf16[32,768]{1,0:T(8,128)(2,1)}, bf16[32,768]{1,0:T(8,128)(2,1)S(1)}, u32[]{:S(2)}) copy-start(bf16[32,768]{1,0:T(8,128)(2,1)S(1)} %collective-permute-done.1.bottom) | copy-start | bytes 147460
  8.3 8.4 %collective-permute-start.3 = (bf16[18,768]{1,0:T(8,128)(2,1)S(1)}, bf16[18,768]{1,0:T(8,128)(2,1)S(1)}, u32[]{:S(2)}, u32[]{:S(2)}) collective-permute-start(bf16[18,768]{1,0:T(8,128)(2,1)S(1)} %pad_maximum_fusion.2), channel_id=1, source_target_pairs={{1,0},{2,1},{3,2},{4,3},{5,4},{6,5},{7,6},{8,7},{9,8},{10,9},{11,1... | collective-permute-start | bytes 82952 | tf_op jit(solution)/shard_map/ppermute | solution.py:36
  12.8 7.1 %collective-permute-start.2 = (bf16[18,768]{1,0:T(8,128)(2,1)S(1)}, bf16[18,768]{1,0:T(8,128)(2,1)S(1)}, u32[]{:S(2)}, u32[]{:S(2)}) collective-permute-start(bf16[18,768]{1,0:T(8,128)(2,1)S(1)} %pad_maximum_fusion.1), channel_id=1, source_target_pairs={{0,1},{1,2},{2,3},{3,4},{4,5},{5,6},{6,7},{7,8},{8,9},{9,10},{10,1... | collective-permute-start | bytes 82952 | tf_op jit(solution)/shard_map/ppermute | solution.py:35
  16.8 3.1 %copy-start.14 = (bf16[18,768]{1,0:T(8,128)(2,1)}, bf16[18,768]{1,0:T(8,128)(2,1)S(1)}, u32[]{:S(2)}) copy-start(bf16[18,768]{1,0:T(8,128)(2,1)S(1)} %collective-permute-done.3.right) | copy-start | bytes 82948
  25.6 12.9 %all-to-all-start = ((bf16[16,8,768]{2,1,0:T(8,128)(2,1)}), bf16[16,8,768]{2,1,0:T(8,128)(2,1)S(1)}, u32[]{:S(2)}, u32[]{:S(2)}) async-start(bf16[16,8,768]{2,1,0:T(8,128)(2,1)} %get-tuple-element.17), calls=%async_computation | async-start | bytes 393216 | tf_op jit(solution)/shard_map/all_to_all | solution.py:407
  38.5 0.7 copy-start.9
  39.2 8.6 %copy-start.4 = (bf16[16,32,768]{2,1,0:T(8,128)(2,1)S(1)}, bf16[16,32,768]{2,1,0:T(8,128)(2,1)}, u32[]{:S(2)}) copy-start(bf16[16,32,768]{2,1,0:T(8,128)(2,1)} %param.13) | copy-start | bytes 2359300
  47.8 2.1 %copy-start.5 = (bf16[512,768]{1,0:T(8,128)(2,1)S(1)}, bf16[512,768]{1,0:T(8,128)(2,1)}, u32[]{:S(2)}) copy-start(bf16[512,768]{1,0:T(8,128)(2,1)} %get-tuple-element.18) | copy-start | bytes 2359300
  47.8 2.1 %copy-start.11 = (bf16[512,768]{1,0:T(8,128)(2,1)S(1)}, bf16[512,768]{1,0:T(8,128)(2,1)}, u32[]{:S(2)}) copy-start(bf16[512,768]{1,0:T(8,128)(2,1)} %get-tuple-element.16) | copy-start | bytes 2359300
  49.9 9.4 %copy-start.1 = (f32[512,768]{1,0:T(8,128)}, f32[512,768]{1,0:T(8,128)S(1)}, u32[]{:S(2)}) copy-start(f32[512,768]{1,0:T(8,128)S(1)} %convert_add_fusion) | copy-start | bytes 4718596
  49.9 1.7 %copy-start.6 = (bf16[512,768]{1,0:T(8,128)(2,1)S(1)}, bf16[512,768]{1,0:T(8,128)(2,1)}, u32[]{:S(2)}) copy-start(bf16[512,768]{1,0:T(8,128)(2,1)} %get-tuple-element.25) | copy-start | bytes 2359300
  53.4 50.0 %collective-permute-start.8 = (bf16[1536,384]{1,0:T(8,128)(2,1)}, bf16[1536,384]{1,0:T(8,128)(2,1)}, u32[]{:S(2)}, u32[]{:S(2)}) collective-permute-start(bf16[1536,384]{1,0:T(8,128)(2,1)} %pad_maximum_fusion), channel_id=1, source_target_pairs={{0,1},{1,0},{2,3},{3,2},{4,5},{5,4},{6,7},{7,6},{8,9},{9,8},{10,11... | collective-permute-start | bytes 3538952 | tf_op jit(solution)/shard_map/ppermute | solution.py:419
  55.1 14.9 %all-to-all-start.1 = ((bf16[16,2,8,768]{3,2,1,0:T(8,128)(2,1)}), bf16[16,2,8,768]{3,2,1,0:T(8,128)(2,1)}, u32[]{:S(2)}, u32[]{:S(2)}) async-start(bf16[16,2,8,768]{3,2,1,0:T(8,128)(2,1)} %get-tuple-element.19), calls=%async_computation.1 | async-start | bytes 786432 | tf_op jit(solution)/shard_map/all_to_all | solution.py:412
  60.0 5.5 %copy-start.10 = (bf16[16,8,768]{2,1,0:T(8,128)(2,1)S(1)}, bf16[16,8,768]{2,1,0:T(8,128)(2,1)}, u32[]{:S(2)}) copy-start(bf16[16,8,768]{2,1,0:T(8,128)(2,1)} %copy-done.9) | copy-start | bytes 589828
  73.5 18.6 %all-to-all-start.3 = ((bf16[128,8,128]{2,1,0:T(8,128)(2,1)}), bf16[128,8,128]{2,1,0:T(8,128)(2,1)}, u32[]{:S(2)}, u32[]{:S(2)}) async-start(bf16[128,8,128]{2,1,0:T(8,128)(2,1)} %get-tuple-element.26), calls=%async_computation.3 | async-start | bytes 524288 | tf_op jit(solution)/shard_map/all_to_all | solution.py:428
  84.4 19.0 %copy-start.3 = (f32[768,384]{1,0:T(8,128)S(1)}, f32[768,384]{1,0:T(8,128)}, u32[]{:S(2)}) copy-start(f32[768,384]{1,0:T(8,128)} %fusion.5) | copy-start | bytes 3538948
  94.0 17.4 %all-to-all-start.4 = ((bf16[8,128,384]{2,1,0:T(8,128)(2,1)}), bf16[8,128,384]{2,1,0:T(8,128)(2,1)}, u32[]{:S(2)}, u32[]{:S(2)}) async-start(bf16[8,128,384]{2,1,0:T(8,128)(2,1)} %broadcast_in_dim.29), calls=%async_computation.4 | async-start | bytes 1572864 | tf_op jit(solution)/shard_map/all_to_all | solution.py:52
  99.1 18.6 %collective-permute-start.4 = (bf16[32,768]{1,0:T(8,128)(2,1)}, bf16[32,768]{1,0:T(8,128)(2,1)}, u32[]{:S(2)}, u32[]{:S(2)}) collective-permute-start(bf16[32,768]{1,0:T(8,128)(2,1)} %get-tuple-element.32), channel_id=1, source_target_pairs={{0,16},{16,32},{32,48},{48,64},{64,80},{80,96},{96,112},{112,0},{1... | collective-permute-start | bytes 147464 | tf_op jit(solution)/shard_map/ppermute | solution.py:35
  101.1 16.7 %collective-permute-start.5 = (bf16[32,768]{1,0:T(8,128)(2,1)}, bf16[32,768]{1,0:T(8,128)(2,1)}, u32[]{:S(2)}, u32[]{:S(2)}) collective-permute-start(bf16[32,768]{1,0:T(8,128)(2,1)} %get-tuple-element.31), channel_id=1, source_target_pairs={{16,0},{32,16},{48,32},{64,48},{80,64},{96,80},{112,96},{0,112},{1... | collective-permute-start | bytes 147464 | tf_op jit(solution)/shard_map/ppermute | solution.py:36
  111.4 6.3 %copy-start.13 = (f32[16,1,768]{2,1,0:T(1,128)S(1)}, f32[16,1,768]{2,1,0:T(1,128)}, u32[]{:S(2)}) copy-start(f32[16,1,768]{2,1,0:T(1,128)} %get-tuple-element.29) | copy-start | bytes 147460
  111.4 6.3 %copy-start.12 = (f32[16,1,768]{2,1,0:T(1,128)S(1)}, f32[16,1,768]{2,1,0:T(1,128)}, u32[]{:S(2)}) copy-start(f32[16,1,768]{2,1,0:T(1,128)} %get-tuple-element.30) | copy-start | bytes 147460
  111.4 25.2 %all-to-all-start.2 = ((bf16[64,24,384]{2,1,0:T(8,128)(2,1)}), bf16[64,24,384]{2,1,0:T(8,128)(2,1)S(1)}, u32[]{:S(2)}, u32[]{:S(2)}) async-start(bf16[64,24,384]{2,1,0:T(8,128)(2,1)} %bitcast.65), calls=%async_computation.2 | async-start | bytes 2359296 | tf_op jit(solution)/shard_map/all_to_all | solution.py:421
  136.7 1.0 copy-start.2
  140.4 21.6 %all-to-all-start.5 = ((bf16[16,24,384]{2,1,0:T(8,128)(2,1)}), bf16[16,24,384]{2,1,0:T(8,128)(2,1)S(1)}, u32[]{:S(2)}, u32[]{:S(2)}) async-start(bf16[16,24,384]{2,1,0:T(8,128)(2,1)} %get-tuple-element.27), calls=%async_computation.5 | async-start | bytes 589824 | tf_op jit(solution)/shard_map/all_to_all | solution.py:446
  144.0 6.3 %collective-permute-start.7 = (bf16[18,768]{1,0:T(8,128)(2,1)S(1)}, bf16[18,768]{1,0:T(8,128)(2,1)S(1)}, u32[]{:S(2)}, u32[]{:S(2)}) collective-permute-start(bf16[18,768]{1,0:T(8,128)(2,1)S(1)} %pad_maximum_fusion.4), channel_id=1, source_target_pairs={{1,0},{2,1},{3,2},{4,3},{5,4},{6,5},{7,6},{8,7},{9,8},{10,9},{11,1... | collective-permute-start | bytes 82952 | tf_op jit(solution)/shard_map/ppermute | solution.py:36
  148.6 12.7 %copy-start.18 = (f32[8,128]{1,0:T(8,128)S(1)}, f32[8,128]{1,0:T(8,128)}, u32[]{:S(2)}) copy-start(f32[8,128]{1,0:T(8,128)} %get-tuple-element.28) | copy-start | bytes 12292
  148.6 7.1 %collective-permute-start.6 = (bf16[18,768]{1,0:T(8,128)(2,1)S(1)}, bf16[18,768]{1,0:T(8,128)(2,1)S(1)}, u32[]{:S(2)}, u32[]{:S(2)}) collective-permute-start(bf16[18,768]{1,0:T(8,128)(2,1)S(1)} %pad_maximum_fusion.3), channel_id=1, source_target_pairs={{0,1},{1,2},{2,3},{3,4},{4,5},{5,6},{6,7},{7,8},{8,9},{9,10},{10,1... | collective-permute-start | bytes 82952 | tf_op jit(solution)/shard_map/ppermute | solution.py:35
  150.3 5.4 %copy-start.16 = (bf16[18,768]{1,0:T(8,128)(2,1)}, bf16[18,768]{1,0:T(8,128)(2,1)S(1)}, u32[]{:S(2)}) copy-start(bf16[18,768]{1,0:T(8,128)(2,1)S(1)} %collective-permute-done.7.right) | copy-start | bytes 82948
  (2 other events, 1.2 us)

commit v3 on v2

--- a/solution.py
+++ b/solution.py
@@ -1,5 +1,3 @@
-from functools import partial
-
 import jax
 import jax.numpy as jnp
 from jax import lax
@@ -7,7 +5,6 @@
 from jax.experimental.pallas import tpu as pltpu
 from jax.sharding import PartitionSpec as P
 
-HEADS = 12
 HD = 64
 POOL = 8
 EPSILON = 1e-05
@@ -45,11 +42,6 @@
     last = jnp.concatenate([up[-1:], tile[:, -1], down[-1:]], axis=0)
     left, right = from_both_sides(first, last, "col")
     return top, bottom, left, right
-
-
-def copy_for_each(x, axis):
-    peers = lax.axis_size(axis)
-    return lax.all_to_all(jnp.broadcast_to(x[None], (peers, *x.shape)), axis, 0, 0, tiled=True)
 
 
 def dot(left, right, dims):
@@ -156,7 +148,9 @@
     )(flags, image, *sides, taps)
 
 
-def attend_kernel(query, dout, cells, w_key, w_value, attended, grad_query, sums):
+def attend_kernel(
+    flags, query, dout, cells, w_key, w_value, attended, grad_query, kept, sent
+):
     low = lax.broadcasted_iota(jnp.int32, (128, LANES), 1) < HD
     all_cells = cells[...]
     zero = jnp.zeros((128, LANES), BF)
@@ -186,36 +180,87 @@
     grad_values = contract_first(weights, d)
     grad_keys = jnp.where(low, grad_keys[:128], grad_keys[128:]) * (HD**-0.5)
     grad_values = jnp.where(low, grad_values[:128], grad_values[128:])
-    sums[:, 0] = grad_keys.astype(BF).reshape(16, 8, LANES)
-    sums[:, 1] = grad_values.astype(BF).reshape(16, 8, LANES)
-
-
-def attend(query, dout, cells, w_key, w_value):
+    odd = flags[5] == 1
+    for i, grad in enumerate((grad_keys, grad_values)):
+        grad = grad.reshape(8, 2, 8, LANES)
+        kept[:, i] = jnp.where(odd, grad[:, 1], grad[:, 0])
+        sent[:, i] = jnp.where(odd, grad[:, 0], grad[:, 1]).astype(BF)
+
+
+def attend(flags, query, dout, cells, w_key, w_value):
     tokens, channels = query.shape
     blocks = channels // LANES
     by_pair = pl.BlockSpec((tokens, LANES), lambda i: (0, i))
     weight = pl.BlockSpec((channels, LANES), lambda i: (0, i))
+    sums = pl.BlockSpec((8, 2, 8, LANES), lambda i: (0, 0, 0, i))
     return pl.pallas_call(
         attend_kernel,
         grid=(blocks,),
         in_specs=[
+            SCALARS,
             by_pair,
             by_pair,
             pl.BlockSpec((128, channels), lambda i: (0, 0)),
             weight,
             weight,
         ],
-        out_specs=[by_pair, by_pair, pl.BlockSpec((16, 2, 8, LANES), lambda i: (0, 0, 0, i))],
+        out_specs=[by_pair, by_pair, sums, sums],
         out_shape=[
             jax.ShapeDtypeStruct((tokens, channels), BF),
             jax.ShapeDtypeStruct((tokens, channels), BF),
-            jax.ShapeDtypeStruct((16, 2, 8, channels), BF),
+            jax.ShapeDtypeStruct((8, 2, 8, channels), F32),
+            jax.ShapeDtypeStruct((8, 2, 8, channels), BF),
         ],
         cost_estimate=pl.CostEstimate(
             flops=3_000_000_000, bytes_accessed=6_000_000, transcendentals=800_000
         ),
         name="attend",
-    )(query, dout, cells, w_key, w_value)
+    )(flags, query, dout, cells, w_key, w_value)
+
+
+def weights_kernel(which, grad_query, flat_grad, hidden, attended, *rest):
+    terms = rest[-1]
+    step = pl.program_id(0)
+
+    def put(value):
+        if len(rest) == 2:
+            value = value + rest[0][...].astype(F32)
+        terms[...] = value.astype(BF)
+
+    @pl.when(step < 2)
+    def _():
+        put(contract_first(grad_query[...], hidden[...]))
+
+    @pl.when(step >= 2)
+    def _():
+        put(contract_first(flat_grad[...], attended[...]))
+
+
+def weight_terms(which, grad_query, flat_grad, hidden, attended, others=None):
+    tokens, channels = hidden.shape
+    half = channels // 2
+    out = pl.BlockSpec((half, half), lambda i, w: (i, 0))
+    operands = [grad_query, flat_grad, hidden, attended] + ([] if others is None else [others])
+    return pl.pallas_call(
+        weights_kernel,
+        grid_spec=pltpu.PrefetchScalarGridSpec(
+            num_scalar_prefetch=1,
+            grid=(4,),
+            in_specs=[
+                pl.BlockSpec((tokens, half), lambda i, w: (0, jnp.minimum(i, 1))),
+                pl.BlockSpec((tokens, half), lambda i, w: (0, jnp.maximum(i - 2, 0))),
+                pl.BlockSpec((tokens, half), lambda i, w: (0, w[0])),
+                pl.BlockSpec((tokens, half), lambda i, w: (0, w[0])),
+            ]
+            + ([] if others is None else [out]),
+            out_specs=out,
+        ),
+        out_shape=jax.ShapeDtypeStruct((2 * channels, half), BF),
+        cost_estimate=pl.CostEstimate(
+            flops=600_000_000, bytes_accessed=4_000_000, transcendentals=0
+        ),
+        name="weight_terms",
+    )(which, *operands)
 
 
 def taps_kernel(flags, image, top, bottom, left, right, early, terms, windows, padded, lines):
@@ -274,8 +319,8 @@
     return pltpu.roll(x[:, base : base + 2 * LANES], base - start + 2 * LANES, 1)[:, :LANES]
 
 
-def cells_kernel(terms, w_key, w_value, standard, inverse, early, windows, grad_pooled, blocks):
-    received = jnp.sum(terms[...].astype(F32), axis=0)
+def cells_kernel(kept, terms, w_key, w_value, standard, inverse, early, windows, grad_pooled, blocks):
+    received = kept[...] + terms[...].astype(F32)
     keys, values = received[0], received[1]
     grad = contract_last(keys.astype(BF), w_key[...]) + contract_last(values.astype(BF), w_value[...])
     own = standard[...]
@@ -303,7 +348,7 @@
             blocks[16 * q + j] = jnp.where(lane < 24, pieces[part, q], rest).astype(BF)
 
 
-def at_cells(terms, w_key, w_value, standard, inverse, early, windows):
+def at_cells(kept, terms, w_key, w_value, standard, inverse, early, windows):
     channels = standard.shape[1]
     return pl.pallas_call(
         cells_kernel,
@@ -313,14 +358,18 @@
         ],
         cost_estimate=pl.CostEstimate(flops=30_000_000, bytes_accessed=3_500_000, transcendentals=0),
         name="at_cells",
-    )(terms, w_key, w_value, standard, inverse, early, windows)
-
-
-def pieces_kernel(flags, got, blocks, cells, placed, conv):
+    )(kept, terms, w_key, w_value, standard, inverse, early, windows)
+
+
+def pieces_kernel(flags, got, blocks, near, far, placed, conv):
     piece = jnp.sum(got[...].astype(F32), axis=0).astype(BF)
-    received = blocks[...]
-    conv[...] = jnp.sum(received.astype(F32), axis=0)
-    cell_piece = contract_first(received.reshape(1024, LANES), cells[...])[:24].astype(BF)
+    conv[...] = jnp.sum(blocks[...].astype(F32), axis=0)
+    total = jnp.zeros((LANES, piece.shape[1]), F32)
+    for i in range(8):
+        row = jnp.bitwise_xor(flags[6], i)
+        own = blocks[pl.ds(row * 16, 16)].reshape(128, LANES)
+        total = total + contract_first(own, near[i] if i < 4 else far[i - 4])
+    cell_piece = total[:24].astype(BF)
     odd = flags[4] == 1
     first = jnp.where(odd, cell_piece, piece)
     second = jnp.where(odd, piece, cell_piece)
@@ -329,19 +378,19 @@
         placed[8 + q] = second
 
 
-def pieces(flags, got, blocks, cells):
-    half = cells.shape[1]
+def pieces(flags, got, blocks, near, far):
+    half = near.shape[2]
     vmem = pl.BlockSpec(memory_space=pltpu.VMEM)
     return pl.pallas_call(
         pieces_kernel,
-        in_specs=[SCALARS, vmem, vmem, vmem],
+        in_specs=[SCALARS, vmem, vmem, vmem, vmem],
         out_shape=[
             jax.ShapeDtypeStruct((16, 24, half), BF),
             jax.ShapeDtypeStruct((8, LANES), F32),
         ],
         cost_estimate=pl.CostEstimate(flops=100_000_000, bytes_accessed=2_500_000, transcendentals=0),
         name="pieces",
-    )(flags, got, blocks, cells)
+    )(flags, got, blocks, near, far)
 
 
 def unmix_kernel(flags, early, pooled, top, bottom, left, right, taps, image, padded):
@@ -384,7 +433,7 @@
     )(flags, early, pooled, *sides, taps)
 
 
-def on_device(image, conv_taps, w_query, w_key, w_value, w_out, grad_out):
+def block_gradients(image, conv_taps, w_query, w_key, w_value, w_out, grad_out):
     height, width, channels = image.shape
     half = channels // 2
     at_row, at_col = lax.axis_index("row"), lax.axis_index("col")
@@ -398,33 +447,42 @@
             at_col > 0,
             at_col < lax.axis_size("col") - 1,
             turned,
+            core == 1,
         ]
     ).astype(jnp.int32)
+    flags = jnp.concatenate([flags, at_row[None].astype(jnp.int32)])
     flat_grad = grad_out.reshape(-1, channels)
     sides = edges_of(image, is_first, is_last)
     dout = contract_last(flat_grad, w_out).astype(BF)
     hidden, standard, inverse, normed = mix(flags, image, sides, conv_taps)
-    cells = lax.all_to_all(normed, "col", 0, 0, tiled=True).reshape(-1, channels)
+    cells = lax.all_to_all(normed, "col", 0, 0, tiled=True)
+    cells = cells.reshape(-1, channels)
     query = jnp.dot(hidden, w_query, preferred_element_type=F32).astype(BF)
-    cells_half = lax.dynamic_slice_in_dim(cells, core * half, half, axis=1)
-    all_cells = copy_for_each(cells_half, "row").reshape(-1, half)
-    attended, grad_query, sums = attend(query, dout, cells, w_key, w_value)
-    terms = lax.all_to_all(sums, "col", 0, 0, tiled=True)
-
-    def half_terms(which):
-        h = lax.dynamic_slice_in_dim(hidden, which * half, half, axis=1)
-        a = lax.dynamic_slice_in_dim(attended, which * half, half, axis=1)
-        return jnp.concatenate([contract_first(grad_query, h), contract_first(flat_grad, a)], axis=0)
-
-    theirs = lax.ppermute(half_terms(1 - core).astype(BF), "col", PAIRS)
-    chip = (half_terms(core) + theirs.astype(F32)).astype(BF)
+    near = lax.dynamic_slice_in_dim(cells, core * half, half, axis=1)[None]
+    for step in range(3):
+        far = lax.ppermute(near, "row", [(i, i ^ (1 << step)) for i in range(8)])
+        if step < 2:
+            near = jnp.concatenate([near, far], axis=0)
+    attended, grad_query, kept, sent = attend(flags, query, dout, cells, w_key, w_value)
+    theirs = weight_terms((1 - core)[None], grad_query, flat_grad, hidden, attended)
+    theirs = lax.ppermute(theirs, "col", PAIRS)
+    chip = weight_terms(core[None], grad_query, flat_grad, hidden, attended, theirs)
     got = lax.all_to_all(
         chip.reshape(64, 24, half), BOTH, 0, 0, tiled=True, axis_index_groups=SUM_GROUPS
     )
+    terms = lax.ppermute(sent, "col", PAIRS)
+    for bit in (1, 2, 3):
+        mine = (at_col >> bit) & 1
+        total = (kept + terms.astype(F32)).reshape(-1, 2, 2, 8, channels)
+        kept = lax.dynamic_index_in_dim(total, mine, 1, keepdims=False)
+        sent = lax.dynamic_index_in_dim(total, 1 - mine, 1, keepdims=False).astype(BF)
+        terms = lax.ppermute(sent, "col", [(j, j ^ (1 << bit)) for j in range(16)])
+    kept, terms = kept[0], terms[0]
     grad_hidden = contract_last(grad_query, w_query)
     early = (flat_grad.astype(F32) + grad_hidden).reshape(height, width, channels)
     early_terms, windows = tap_terms(flags, image, sides, early)
-    pooled, block = at_cells(terms, w_key, w_value, standard, inverse, early_terms, windows)
+    pooled, block = at_cells(kept, terms, w_key, w_value, standard, inverse, early_terms, windows)
+    block, got = lax.optimization_barrier((block, got))
     blocks = lax.all_to_all(block, BOTH, 0, 0, tiled=True)
     rows = jnp.repeat(pooled, POOL, axis=0).reshape(2, width, channels)
     up = jnp.concatenate([pooled[0:1], pooled[4:5]], axis=0)
@@ -442,7 +500,7 @@
         "col",
     )
     grad_image = unmix(flags, early, pooled, (top, bottom, left, right), conv_taps)
-    placed, conv = pieces(flags, got, blocks, all_cells)
+    placed, conv = pieces(flags, got, blocks, near, far)
     placed = lax.all_to_all(
         placed, BOTH, 0, 0, tiled=True, axis_index_groups=PLACE_GROUPS
     )
@@ -453,7 +511,7 @@
 
 def solution(mesh):
     return jax.shard_map(
-        on_device,
+        block_gradients,
         mesh=mesh,
         in_specs=(P("row", "col", None), P(), P(), P(), P(), P(), P("row", "col", None)),
         out_specs=(P("row", "col", None), P(None, "col"), P(None, "col")),

time: 165 us -> 162 us (0.982)
  the two profiles are of different devices: /device:TPU:0 before, /device:TPU:96 now
where the time goes in v3:
time: 162 us; the launch traced here: 160 us
  starting transfers between devices  49.6 us (31%)
  waiting for transfers between devices  42.7 us (26%)
  Pallas kernels  40 us (25%)
  local copies, waits for them, and re-layouts  13.4 us (8%)
  matrix products  9.14 us (6%)
  other arithmetic  3.7 us (2%)
    all_to_all x1, waiting for transfers between devices, block_gradients(): lax.all_to_all(chip.reshape(64, 24, half), BOTH, 0, 0, tiled=True, axis_i...  12.9 us
    ppermute x4, waiting for transfers between devices, from_both_sides(): lax.ppermute(last, axis, [(i, (i + 1) % count) for i in range(count)])  10.7 us
    pallas_call x2, Pallas kernels, weight_terms(): pl.pallas_call(weights_kernel, grid_spec=pltpu.PrefetchScalarGridSpec(num...  9.45 us
    ppermute x4, starting transfers between devices, from_both_sides(): lax.ppermute(first, axis, [((i + 1) % count, i) for i in range(count)])  8.95 us
    all_to_all x1, starting transfers between devices, block_gradients(): lax.all_to_all(chip.reshape(64, 24, half), BOTH, 0, 0, tiled=True, axis_i...  8.89 us
    pallas_call x1, Pallas kernels, attend(): pl.pallas_call(attend_kernel, grid=(blocks,), in_specs=[SCALARS, by_pair,...  8.63 us
    all_to_all x1, starting transfers between devices, block_gradients(): blocks = lax.all_to_all(block, BOTH, 0, 0, tiled=True)  8.06 us
    ppermute x3, waiting for transfers between devices, block_gradients(): terms = lax.ppermute(sent, 'col', [(j, j ^ 1 << bit) for j in range(16)])  6.4 us
  transfers between devices with their start and end apart: 20, of which 11 were waited for; matrix products, arithmetic and copies ran while one was open for 11% of the time, Pallas kernels for 12%

profile of v3, /device:TPU:96, one launch (start us, length us, event | category | flops | bytes accessed | tf_op | source)
XLA Modules:
  0.0 159.6 jit_solution(16903479166232244919)
XLA Ops:
  1.6 1.4 collective-permute-start
  3.6 3.2 %convolution_convert_fusion.dout = bf16[512,768]{1,0:T(8,128)(2,1)} fusion(bf16[512,768]{1,0:T(8,128)(2,1)} %bitcast.84, bf16[768,768]{1,0:T(8,128)(2,1)} %param.12), kind=kOutput, calls=%fused_computation.1 | convolution fusion | flops 604372992 | bytes 2752512 | tf_op jit(solution)/shard_map/dot_general | solution.py:48
  8.3 1.9 %collective-permute-start.3 = (bf16[18,768]{1,0:T(8,128)(2,1)S(1)}, bf16[18,768]{1,0:T(8,128)(2,1)S(1)}, u32[]{:S(2)}, u32[]{:S(2)}) collective-permute-start(bf16[18,768]{1,0:T(8,128)(2,1)S(1)} %pad_maximum_fusion.3), channel_id=1, source_target_pairs={{1,0},{2,1},{3,2},{4,3},{5,4},{6,5},{7,6},{8,7},{9,8},{10,9},{11,1... | collective-permute-start | bytes 82952 | tf_op jit(solution)/shard_map/ppermute | solution.py:33
  11.9 5.4 %collective-permute-done.2.left = bf16[18,768]{1,0:T(8,128)(2,1)S(1)} collective-permute-done((bf16[18,768]{1,0:T(8,128)(2,1)S(1)}, bf16[18,768]{1,0:T(8,128)(2,1)S(1)}, u32[]{:S(2)}, u32[]{:S(2)}) %collective-permute-start.2) | collective-permute-done | bytes 27680 | tf_op jit(solution)/shard_map/ppermute | solution.py:32
  17.9 5.2 %mix.1 = (bf16[512,768]{1,0:T(8,128)(2,1)}, f32[8,768]{1,0:T(8,128)}, f32[8,128]{1,0:T(8,128)}, bf16[16,8,768]{2,1,0:T(8,128)(2,1)}) custom-call(s32[7]{0:T(128)} %pad_add_fusion.flags, bf16[16,32,768]{2,1,0:T(8,128)(2,1)} %image.3, bf16[32,768]{1,0:T(8,128)(2,1)} %copy-done.6, bf16[32,768]{1,0:T(8,128)(2,1)} %copy-done.7, bf16[18,768]{1,0:T(8,128)(2,1)} %copy-done.18, ...), custom_call_target="tpu_custom_call" | custom-call | flops 8000000 | bytes 2000000 | tf_op jit(solution)/shard_map/mix/pallas_call | solution.py:124
  23.1 6.3 %all-to-all-start = ((bf16[16,8,768]{2,1,0:T(8,128)(2,1)}), bf16[16,8,768]{2,1,0:T(8,128)(2,1)S(1)}, u32[]{:S(2)}, u32[]{:S(2)}) async-start(bf16[16,8,768]{2,1,0:T(8,128)(2,1)} %get-tuple-element.20), calls=%async_computation | async-start | bytes 393216 | tf_op jit(solution)/shard_map/all_to_all | solution.py:458
  29.5 2.8 %convolution_convert_fusion.1.query = bf16[512,768]{1,0:T(8,128)(2,1)} fusion(bf16[512,768]{1,0:T(8,128)(2,1)} %get-tuple-element.19.hidden, bf16[768,768]{1,0:T(8,128)(2,1)S(1)} %copy-done), kind=kOutput, calls=%fused_computation.2 | convolution fusion | flops 604372992 | bytes 2752512 | tf_op jit(solution)/shard_map/dot_general | solution.py:460
  32.3 2.9 %all-to-all-done = bf16[16,8,768]{2,1,0:T(8,128)(2,1)S(1)} async-done(((bf16[16,8,768]{2,1,0:T(8,128)(2,1)}), bf16[16,8,768]{2,1,0:T(8,128)(2,1)S(1)}, u32[]{:S(2)}, u32[]{:S(2)}) %all-to-all-start) | async-done | bytes 196640 | tf_op jit(solution)/shard_map/all_to_all | solution.py:458
  35.8 8.6 %attend.1 = (bf16[512,768]{1,0:T(8,128)(2,1)}, bf16[512,768]{1,0:T(8,128)(2,1)}, f32[8,2,8,768]{3,2,1,0:T(8,128)}, bf16[8,2,8,768]{3,2,1,0:T(8,128)(2,1)}) custom-call(s32[7]{0:T(128)} %pad_add_fusion.flags, bf16[512,768]{1,0:T(8,128)(2,1)} %convolution_convert_fusion.1.query, bf16[512,768]{1,0:T(8,128)(2,1)} %convolution_convert_fusion.dout, ...), custom_call_target="tpu_custom_call" | custom-call | flops 3000000000 | bytes 6000000 | tf_op jit(solution)/shard_map/attend/pallas_call | solution.py:196
  44.5 3.1 %convert_add_fusion = f32[512,768]{1,0:T(8,128)} fusion(bf16[512,768]{1,0:T(8,128)(2,1)S(1)} %bitcast.87, bf16[512,768]{1,0:T(8,128)(2,1)} %get-tuple-element.21.grad_query, bf16[768,768]{1,0:T(8,128)(2,1)S(1)} %copy-done), kind=kOutput, calls=%fused_computation | convolution fusion | flops 604766208 | bytes 4325376 | tf_op jit(solution)/shard_map/dot_general | solution.py:48
  47.6 4.7 %weight_terms.2 = bf16[1536,384]{1,0:T(8,128)(2,1)} custom-call(s32[1]{0:T(128)} %bitcast.29.which, bf16[512,768]{1,0:T(8,128)(2,1)} %get-tuple-element.21.grad_query, bf16[512,768]{1,0:T(8,128)(2,1)} %bitcast.85, bf16[512,768]{1,0:T(8,128)(2,1)} %get-tuple-element.19.hidden, bf16[512,768]{1,0:T(8,128)(2,1)} %get-tuple-element.30.attended), custom_call_target="tpu_custom_call" | custom-call | flops 600000000 | bytes 4000000 | tf_op jit(solution)/shard_map/weight_terms/pallas_call | solution.py:244
  52.8 2.6 %collective-permute-start.13 = (bf16[1,128,384]{2,1,0:T(8,128)(2,1)S(1)}, bf16[1,128,384]{2,1,0:T(8,128)(2,1)S(1)}, u32[]{:S(2)}, u32[]{:S(2)}) collective-permute-start(bf16[1,128,384]{2,1,0:T(8,128)(2,1)S(1)} %dynamic-slice_bitcast_fusion), channel_id=1, source_target_pairs={{0,16},{16,0},{32,48},{48,32},{64,80},{80,64},{96,112},{112,96},{1... | collective-permute-start | bytes 294920 | tf_op jit(solution)/shard_map/ppermute | solution.py:463
  55.4 5.5 %tap_terms.1 = (f32[9,768]{1,0:T(8,128)}, f32[9,8,768]{2,1,0:T(8,128)}) custom-call(s32[7]{0:T(128)} %pad_add_fusion.flags, bf16[16,32,768]{2,1,0:T(8,128)(2,1)} %image.3, bf16[32,768]{1,0:T(8,128)(2,1)} %copy-done.6, bf16[32,768]{1,0:T(8,128)(2,1)} %copy-done.7, bf16[18,768]{1,0:T(8,128)(2,1)} %copy-done.18, bf16[18,768]{1,0:T(8,128)(2,1)} %copy-done.17, ...), custom_call_target="tpu_custom_call" | custom-call | flops 8000000 | bytes 3000000 | tf_op jit(solution)/shard_map/tap_terms/pallas_call | solution.py:297
  60.9 1.8 %fusion.8 = (f32[16,1,768]{2,1,0:T(1,128)}, f32[16,1,768]{2,1,0:T(1,128)}) fusion(f32[16,32,768]{2,1,0:T(8,128)} %bitcast.81), kind=kLoop, calls=%fused_computation.42 | loop fusion | bytes 196608 | tf_op jit(solution)/shard_map/slice | solution.py:493
  63.7 3.9 %collective-permute-done.5 = bf16[4,2,8,768]{3,2,1,0:T(8,128)(2,1)S(1)} collective-permute-done((bf16[4,2,8,768]{3,2,1,0:T(8,128)(2,1)S(1)}, bf16[4,2,8,768]{3,2,1,0:T(8,128)(2,1)S(1)}, u32[]{:S(2)}, u32[]{:S(2)}) %collective-permute-start.5) | collective-permute-done | bytes 98336 | tf_op jit(solution)/shard_map/ppermute | solution.py:479
  67.7 1.4 collective-permute-start.6
  70.2 1.9 %collective-permute-start.15 = (bf16[4,128,384]{2,1,0:T(8,128)(2,1)S(1)}, bf16[4,128,384]{2,1,0:T(8,128)(2,1)S(1)}, u32[]{:S(2)}, u32[]{:S(2)}) collective-permute-start(bf16[4,128,384]{2,1,0:T(8,128)(2,1)S(1)} %pad_maximum_fusion.near), channel_id=1, source_target_pairs={{0,64},{16,80},{32,96},{48,112},{64,0},{80,16},{96,32},{112,48},{1... | collective-permute-start | bytes 1179656 | tf_op jit(solution)/shard_map/ppermute | solution.py:463
  73.4 3.6 %collective-permute-start.7 = (bf16[1,2,8,768]{3,2,1,0:T(8,128)(2,1)S(1)}, bf16[1,2,8,768]{3,2,1,0:T(8,128)(2,1)S(1)}, u32[]{:S(2)}, u32[]{:S(2)}) collective-permute-start(bf16[1,2,8,768]{3,2,1,0:T(8,128)(2,1)S(1)} %dynamic-slice_convert_fusion), channel_id=1, source_target_pairs={{0,8},{1,9},{2,10},{3,11},{4,12},{5,13},{6,14},{7,15},{8,0},{9,1},... | collective-permute-start | bytes 73736 | tf_op jit(solution)/shard_map/ppermute | solution.py:479
  79.4 3.5 %at_cells.1 = (f32[8,768]{1,0:T(8,128)}, bf16[128,8,128]{2,1,0:T(8,128)(2,1)}) custom-call(f32[2,8,768]{2,1,0:T(8,128)} %dynamic-slice_bitcast_fusion.1.kept, bf16[2,8,768]{2,1,0:T(8,128)(2,1)} %bitcast.98, bf16[768,768]{1,0:T(8,128)(2,1)} %w_key.3, bf16[768,768]{1,0:T(8,128)(2,1)} %w_value.3, f32[8,768]{1,0:T(8,128)} %get-tuple-element.24.standard, ...), custom_call_target="tpu_custom_call" | custom-call | flops 30000000 | bytes 3500000 | tf_op jit(solution)/shard_map/at_cells/pallas_call | solution.py:353
  85.1 1.6 %collective-permute-start.9 = (bf16[32,768]{1,0:T(8,128)(2,1)S(1)}, bf16[32,768]{1,0:T(8,128)(2,1)S(1)}, u32[]{:S(2)}, u32[]{:S(2)}) collective-permute-start(bf16[32,768]{1,0:T(8,128)(2,1)S(1)} %get-tuple-element.37), channel_id=1, source_target_pairs={{16,0},{32,16},{48,32},{64,48},{80,64},{96,80},{112,96},{0,112},{1... | collective-permute-start | bytes 147464 | tf_op jit(solution)/shard_map/ppermute | solution.py:33
  87.8 4.8 %weight_terms.3 = bf16[1536,384]{1,0:T(8,128)(2,1)} custom-call(s32[1]{0:T(128)} %bitcast.28.which, bf16[512,768]{1,0:T(8,128)(2,1)} %get-tuple-element.21.grad_query, bf16[512,768]{1,0:T(8,128)(2,1)} %bitcast.86, bf16[512,768]{1,0:T(8,128)(2,1)} %get-tuple-element.19.hidden, bf16[512,768]{1,0:T(8,128)(2,1)} %get-tuple-element.30.attended, ...), custom_call_target="tpu_custom_call" | custom-call | flops 600000000 | bytes 4000000 | tf_op jit(solution)/shard_map/weight_terms/pallas_call | solution.py:244
  92.6 8.9 %all-to-all-start.1 = ((bf16[64,24,384]{2,1,0:T(8,128)(2,1)}), bf16[64,24,384]{2,1,0:T(8,128)(2,1)S(1)}, u32[]{:S(2)}, u32[]{:S(2)}) async-start(bf16[64,24,384]{2,1,0:T(8,128)(2,1)} %bitcast.83), calls=%async_computation.1 | async-start | bytes 2359296 | tf_op jit(solution)/shard_map/all_to_all | solution.py:470
  102.9 12.9 %all-to-all-done.1.got = bf16[64,24,384]{2,1,0:T(8,128)(2,1)S(1)} async-done(((bf16[64,24,384]{2,1,0:T(8,128)(2,1)}), bf16[64,24,384]{2,1,0:T(8,128)(2,1)S(1)}, u32[]{:S(2)}, u32[]{:S(2)}) %all-to-all-start.1) | async-done | bytes 1179680 | tf_op jit(solution)/shard_map/all_to_all | solution.py:470
  115.8 8.1 %all-to-all-start.2 = ((bf16[128,8,128]{2,1,0:T(8,128)(2,1)}), bf16[128,8,128]{2,1,0:T(8,128)(2,1)S(1)}, u32[]{:S(2)}, u32[]{:S(2)}) async-start(bf16[128,8,128]{2,1,0:T(8,128)(2,1)} %get-tuple-element.32), calls=%async_computation.2 | async-start | bytes 524288 | tf_op jit(solution)/shard_map/all_to_all | solution.py:486
  123.9 1.3 fusion.10
  126.6 6.0 %all-to-all-done.2.blocks = bf16[128,8,128]{2,1,0:T(8,128)(2,1)S(1)} async-done(((bf16[128,8,128]{2,1,0:T(8,128)(2,1)}), bf16[128,8,128]{2,1,0:T(8,128)(2,1)S(1)}, u32[]{:S(2)}, u32[]{:S(2)}) %all-to-all-start.2) | async-done | bytes 262176 | tf_op jit(solution)/shard_map/all_to_all | solution.py:486
  133.2 2.7 %pieces.1 = (bf16[16,24,384]{2,1,0:T(8,128)(2,1)}, f32[8,128]{1,0:T(8,128)}) custom-call(s32[7]{0:T(128)} %pad_add_fusion.flags, bf16[64,24,384]{2,1,0:T(8,128)(2,1)} %copy-done.1, bf16[128,8,128]{2,1,0:T(8,128)(2,1)} %copy-done.5, bf16[4,128,384]{2,1,0:T(8,128)(2,1)} %copy-done.3, bf16[4,128,384]{2,1,0:T(8,128)(2,1)} %copy-done.10), custom_call_target="tpu_custom_call" | custom-call | flops 100000000 | bytes 2500000 | tf_op jit(solution)/shard_map/pieces/pallas_call | solution.py:384
  136.0 4.6 %all-to-all-start.3 = ((bf16[16,24,384]{2,1,0:T(8,128)(2,1)}), bf16[16,24,384]{2,1,0:T(8,128)(2,1)S(1)}, u32[]{:S(2)}, u32[]{:S(2)}) async-start(bf16[16,24,384]{2,1,0:T(8,128)(2,1)} %get-tuple-element.33), calls=%async_computation.3 | async-start | bytes 589824 | tf_op jit(solution)/shard_map/all_to_all | solution.py:504
  140.6 4.7 %collective-permute-start.11 = (bf16[18,768]{1,0:T(8,128)(2,1)S(1)}, bf16[18,768]{1,0:T(8,128)(2,1)S(1)}, u32[]{:S(2)}, u32[]{:S(2)}) collective-permute-start(bf16[18,768]{1,0:T(8,128)(2,1)S(1)} %pad_maximum_fusion.5), channel_id=1, source_target_pairs={{1,0},{2,1},{3,2},{4,3},{5,4},{6,5},{7,6},{8,7},{9,8},{10,9},{11,1... | collective-permute-start | bytes 82952 | tf_op jit(solution)/shard_map/ppermute | solution.py:33
  145.4 1.8 %collective-permute-done.11.right = bf16[18,768]{1,0:T(8,128)(2,1)S(1)} collective-permute-done((bf16[18,768]{1,0:T(8,128)(2,1)S(1)}, bf16[18,768]{1,0:T(8,128)(2,1)S(1)}, u32[]{:S(2)}, u32[]{:S(2)}) %collective-permute-start.11) | collective-permute-done | bytes 27680 | tf_op jit(solution)/shard_map/ppermute | solution.py:33
  147.1 5.2 %collective-permute-done.10.left = bf16[18,768]{1,0:T(8,128)(2,1)S(1)} collective-permute-done((bf16[18,768]{1,0:T(8,128)(2,1)S(1)}, bf16[18,768]{1,0:T(8,128)(2,1)S(1)}, u32[]{:S(2)}, u32[]{:S(2)}) %collective-permute-start.10) | collective-permute-done | bytes 27680 | tf_op jit(solution)/shard_map/ppermute | solution.py:32
  153.0 5.0 %unmix.1 = bf16[16,32,768]{2,1,0:T(8,128)(2,1)} custom-call(s32[7]{0:T(128)} %pad_add_fusion.flags, f32[16,32,768]{2,1,0:T(8,128)} %bitcast.82, f32[8,768]{1,0:T(8,128)} %get-tuple-element.28.pooled, bf16[32,768]{1,0:T(8,128)(2,1)} %copy-done.14, bf16[32,768]{1,0:T(8,128)(2,1)} %copy-done.15, bf16[18,768]{1,0:T(8,128)(2,1)} %copy-done.20, ...), custom_call_target="tpu_custom_call" | custom-call | flops 8000000 | bytes 3000000 | tf_op jit(solution)/shard_map/unmix/pallas_call | solution.py:418
  (116 shorter events, 21.2 us)
Async XLA Ops:
  0.6 28.9 %copy-start = (bf16[768,768]{1,0:T(8,128)(2,1)S(1)}, bf16[768,768]{1,0:T(8,128)(2,1)}, u32[]{:S(2)}) copy-start(bf16[768,768]{1,0:T(8,128)(2,1)} %param.9) | copy-start | bytes 3538948
  1.6 6.6 %collective-permute-start = (bf16[32,768]{1,0:T(8,128)(2,1)S(1)}, bf16[32,768]{1,0:T(8,128)(2,1)S(1)}, u32[]{:S(2)}, u32[]{:S(2)}) collective-permute-start(bf16[32,768]{1,0:T(8,128)(2,1)S(1)} %get-tuple-element.42), channel_id=1, source_target_pairs={{0,16},{16,32},{32,48},{48,64},{64,80},{80,96},{96,112},{112,0},{1... | collective-permute-start | bytes 147464 | tf_op jit(solution)/shard_map/ppermute | solution.py:32
  3.0 5.3 %collective-permute-start.1 = (bf16[32,768]{1,0:T(8,128)(2,1)S(1)}, bf16[32,768]{1,0:T(8,128)(2,1)S(1)}, u32[]{:S(2)}, u32[]{:S(2)}) collective-permute-start(bf16[32,768]{1,0:T(8,128)(2,1)S(1)} %get-tuple-element.41), channel_id=1, source_target_pairs={{16,0},{32,16},{48,32},{64,48},{80,64},{96,80},{112,96},{0,112},{1... | collective-permute-start | bytes 147464 | tf_op jit(solution)/shard_map/ppermute | solution.py:33
  8.2 9.2 %copy-start.6 = (bf16[32,768]{1,0:T(8,128)(2,1)}, bf16[32,768]{1,0:T(8,128)(2,1)S(1)}, u32[]{:S(2)}) copy-start(bf16[32,768]{1,0:T(8,128)(2,1)S(1)} %collective-permute-done.top) | copy-start | bytes 147460
  8.2 9.1 %copy-start.7 = (bf16[32,768]{1,0:T(8,128)(2,1)}, bf16[32,768]{1,0:T(8,128)(2,1)S(1)}, u32[]{:S(2)}) copy-start(bf16[32,768]{1,0:T(8,128)(2,1)S(1)} %collective-permute-done.1.bottom) | copy-start | bytes 147460
  8.3 3.6 %collective-permute-start.3 = (bf16[18,768]{1,0:T(8,128)(2,1)S(1)}, bf16[18,768]{1,0:T(8,128)(2,1)S(1)}, u32[]{:S(2)}, u32[]{:S(2)}) collective-permute-start(bf16[18,768]{1,0:T(8,128)(2,1)S(1)} %pad_maximum_fusion.3), channel_id=1, source_target_pairs={{1,0},{2,1},{3,2},{4,3},{5,4},{6,5},{7,6},{8,7},{9,8},{10,9},{11,1... | collective-permute-start | bytes 82952 | tf_op jit(solution)/shard_map/ppermute | solution.py:33
  10.3 7.1 %collective-permute-start.2 = (bf16[18,768]{1,0:T(8,128)(2,1)S(1)}, bf16[18,768]{1,0:T(8,128)(2,1)S(1)}, u32[]{:S(2)}, u32[]{:S(2)}) collective-permute-start(bf16[18,768]{1,0:T(8,128)(2,1)S(1)} %pad_maximum_fusion.2), channel_id=1, source_target_pairs={{0,1},{1,2},{2,3},{3,4},{4,5},{5,6},{6,7},{7,8},{8,9},{9,10},{10,1... | collective-permute-start | bytes 82952 | tf_op jit(solution)/shard_map/ppermute | solution.py:32
  23.1 12.0 %all-to-all-start = ((bf16[16,8,768]{2,1,0:T(8,128)(2,1)}), bf16[16,8,768]{2,1,0:T(8,128)(2,1)S(1)}, u32[]{:S(2)}, u32[]{:S(2)}) async-start(bf16[16,8,768]{2,1,0:T(8,128)(2,1)} %get-tuple-element.20), calls=%async_computation | async-start | bytes 393216 | tf_op jit(solution)/shard_map/all_to_all | solution.py:458
  52.2 34.5 %collective-permute-start.12 = (bf16[1536,384]{1,0:T(8,128)(2,1)}, bf16[1536,384]{1,0:T(8,128)(2,1)S(1)}, u32[]{:S(2)}, u32[]{:S(2)}) collective-permute-start(bf16[1536,384]{1,0:T(8,128)(2,1)} %weight_terms.2), channel_id=1, source_target_pairs={{0,1},{1,0},{2,3},{3,2},{4,5},{5,4},{6,7},{7,6},{8,9},{9,8},{10,11... | collective-permute-start | bytes 3538952 | tf_op jit(solution)/shard_map/ppermute | solution.py:468
  52.5 10.2 %collective-permute-start.4 = (bf16[8,2,8,768]{3,2,1,0:T(8,128)(2,1)S(1)}, bf16[8,2,8,768]{3,2,1,0:T(8,128)(2,1)S(1)}, u32[]{:S(2)}, u32[]{:S(2)}) collective-permute-start(bf16[8,2,8,768]{3,2,1,0:T(8,128)(2,1)S(1)} %copy-done.27), channel_id=1, source_target_pairs={{0,1},{1,0},{2,3},{3,2},{4,5},{5,4},{6,7},{7,6},{8,9},{9,8},{10,11... | collective-permute-start | bytes 589832 | tf_op jit(solution)/shard_map/ppermute | solution.py:473
  52.8 10.6 %collective-permute-start.13 = (bf16[1,128,384]{2,1,0:T(8,128)(2,1)S(1)}, bf16[1,128,384]{2,1,0:T(8,128)(2,1)S(1)}, u32[]{:S(2)}, u32[]{:S(2)}) collective-permute-start(bf16[1,128,384]{2,1,0:T(8,128)(2,1)S(1)} %dynamic-slice_bitcast_fusion), channel_id=1, source_target_pairs={{0,16},{16,0},{32,48},{48,32},{64,80},{80,64},{96,112},{112,96},{1... | collective-permute-start | bytes 294920 | tf_op jit(solution)/shard_map/ppermute | solution.py:463
  62.8 4.8 %collective-permute-start.5 = (bf16[4,2,8,768]{3,2,1,0:T(8,128)(2,1)S(1)}, bf16[4,2,8,768]{3,2,1,0:T(8,128)(2,1)S(1)}, u32[]{:S(2)}, u32[]{:S(2)}) collective-permute-start(bf16[4,2,8,768]{3,2,1,0:T(8,128)(2,1)S(1)} %fusion), channel_id=1, source_target_pairs={{0,2},{1,3},{2,0},{3,1},{4,6},{5,7},{6,4},{7,5},{8,10},{9,11},{10,... | collective-permute-start | bytes 294920 | tf_op jit(solution)/shard_map/ppermute | solution.py:479
  63.4 6.8 %collective-permute-start.14 = (bf16[2,128,384]{2,1,0:T(8,128)(2,1)S(1)}, bf16[2,128,384]{2,1,0:T(8,128)(2,1)S(1)}, u32[]{:S(2)}, u32[]{:S(2)}) collective-permute-start(bf16[2,128,384]{2,1,0:T(8,128)(2,1)S(1)} %pad_maximum_fusion.1), channel_id=1, source_target_pairs={{0,32},{16,48},{32,0},{48,16},{64,96},{80,112},{96,64},{112,80},{1... | collective-permute-start | bytes 589832 | tf_op jit(solution)/shard_map/ppermute | solution.py:463
  67.7 5.7 %collective-permute-start.6 = (bf16[2,2,8,768]{3,2,1,0:T(8,128)(2,1)S(1)}, bf16[2,2,8,768]{3,2,1,0:T(8,128)(2,1)S(1)}, u32[]{:S(2)}, u32[]{:S(2)}) collective-permute-start(bf16[2,2,8,768]{3,2,1,0:T(8,128)(2,1)S(1)} %fusion.3), channel_id=1, source_target_pairs={{0,4},{1,5},{2,6},{3,7},{4,0},{5,1},{6,2},{7,3},{8,12},{9,13},{10,... | collective-permute-start | bytes 147464 | tf_op jit(solution)/shard_map/ppermute | solution.py:479
  70.2 12.7 %copy-start.3 = (bf16[4,128,384]{2,1,0:T(8,128)(2,1)}, bf16[4,128,384]{2,1,0:T(8,128)(2,1)S(1)}, u32[]{:S(2)}) copy-start(bf16[4,128,384]{2,1,0:T(8,128)(2,1)S(1)} %pad_maximum_fusion.near) | copy-start | bytes 1179652
  70.2 56.3 %collective-permute-start.15 = (bf16[4,128,384]{2,1,0:T(8,128)(2,1)S(1)}, bf16[4,128,384]{2,1,0:T(8,128)(2,1)S(1)}, u32[]{:S(2)}, u32[]{:S(2)}) collective-permute-start(bf16[4,128,384]{2,1,0:T(8,128)(2,1)S(1)} %pad_maximum_fusion.near), channel_id=1, source_target_pairs={{0,64},{16,80},{32,96},{48,112},{64,0},{80,16},{96,32},{112,48},{1... | collective-permute-start | bytes 1179656 | tf_op jit(solution)/shard_map/ppermute | solution.py:463
  73.4 5.4 %collective-permute-start.7 = (bf16[1,2,8,768]{3,2,1,0:T(8,128)(2,1)S(1)}, bf16[1,2,8,768]{3,2,1,0:T(8,128)(2,1)S(1)}, u32[]{:S(2)}, u32[]{:S(2)}) collective-permute-start(bf16[1,2,8,768]{3,2,1,0:T(8,128)(2,1)S(1)} %dynamic-slice_convert_fusion), channel_id=1, source_target_pairs={{0,8},{1,9},{2,10},{3,11},{4,12},{5,13},{6,14},{7,15},{8,0},{9,1},... | collective-permute-start | bytes 73736 | tf_op jit(solution)/shard_map/ppermute | solution.py:479
  84.7 16.9 %collective-permute-start.8 = (bf16[32,768]{1,0:T(8,128)(2,1)S(1)}, bf16[32,768]{1,0:T(8,128)(2,1)S(1)}, u32[]{:S(2)}, u32[]{:S(2)}) collective-permute-start(bf16[32,768]{1,0:T(8,128)(2,1)S(1)} %get-tuple-element.38), channel_id=1, source_target_pairs={{0,16},{16,32},{32,48},{48,64},{64,80},{80,96},{96,112},{112,0},{1... | collective-permute-start | bytes 147464 | tf_op jit(solution)/shard_map/ppermute | solution.py:32
  85.1 17.1 %collective-permute-start.9 = (bf16[32,768]{1,0:T(8,128)(2,1)S(1)}, bf16[32,768]{1,0:T(8,128)(2,1)S(1)}, u32[]{:S(2)}, u32[]{:S(2)}) collective-permute-start(bf16[32,768]{1,0:T(8,128)(2,1)S(1)} %get-tuple-element.37), channel_id=1, source_target_pairs={{16,0},{32,16},{48,32},{64,48},{80,64},{96,80},{112,96},{0,112},{1... | collective-permute-start | bytes 147464 | tf_op jit(solution)/shard_map/ppermute | solution.py:33
  92.6 23.2 %all-to-all-start.1 = ((bf16[64,24,384]{2,1,0:T(8,128)(2,1)}), bf16[64,24,384]{2,1,0:T(8,128)(2,1)S(1)}, u32[]{:S(2)}, u32[]{:S(2)}) async-start(bf16[64,24,384]{2,1,0:T(8,128)(2,1)} %bitcast.83), calls=%async_computation.1 | async-start | bytes 2359296 | tf_op jit(solution)/shard_map/all_to_all | solution.py:470
  101.6 34.3 %copy-start.14 = (bf16[32,768]{1,0:T(8,128)(2,1)}, bf16[32,768]{1,0:T(8,128)(2,1)S(1)}, u32[]{:S(2)}) copy-start(bf16[32,768]{1,0:T(8,128)(2,1)S(1)} %collective-permute-done.8.top) | copy-start | bytes 147460
  102.3 33.7 %copy-start.15 = (bf16[32,768]{1,0:T(8,128)(2,1)}, bf16[32,768]{1,0:T(8,128)(2,1)S(1)}, u32[]{:S(2)}) copy-start(bf16[32,768]{1,0:T(8,128)(2,1)S(1)} %collective-permute-done.9.bottom) | copy-start | bytes 147460
  115.8 16.7 %copy-start.1 = (bf16[64,24,384]{2,1,0:T(8,128)(2,1)}, bf16[64,24,384]{2,1,0:T(8,128)(2,1)S(1)}, u32[]{:S(2)}) copy-start(bf16[64,24,384]{2,1,0:T(8,128)(2,1)S(1)} %all-to-all-done.1.got) | copy-start | bytes 3538948
  115.8 16.7 %all-to-all-start.2 = ((bf16[128,8,128]{2,1,0:T(8,128)(2,1)}), bf16[128,8,128]{2,1,0:T(8,128)(2,1)S(1)}, u32[]{:S(2)}, u32[]{:S(2)}) async-start(bf16[128,8,128]{2,1,0:T(8,128)(2,1)} %get-tuple-element.32), calls=%async_computation.2 | async-start | bytes 524288 | tf_op jit(solution)/shard_map/all_to_all | solution.py:486
  126.5 14.0 %copy-start.24 = (bf16[1,768]{1,0:T(2,128)(2,1)S(1)}, bf16[1,768]{1,0:T(2,128)(2,1)}, u32[]{:S(2)}) copy-start(bf16[1,768]{1,0:T(2,128)(2,1)} %get-tuple-element.43) | copy-start | bytes 4612
  126.6 14.0 %copy-start.25 = (bf16[1,768]{1,0:T(2,128)(2,1)S(1)}, bf16[1,768]{1,0:T(2,128)(2,1)}, u32[]{:S(2)}) copy-start(bf16[1,768]{1,0:T(2,128)(2,1)} %get-tuple-element.45) | copy-start | bytes 4612
  126.6 18.7 %copy-start.22 = (bf16[1,768]{1,0:T(2,128)(2,1)S(1)}, bf16[1,768]{1,0:T(2,128)(2,1)}, u32[]{:S(2)}) copy-start(bf16[1,768]{1,0:T(2,128)(2,1)} %get-tuple-element.44) | copy-start | bytes 4612
  126.6 18.7 %copy-start.23 = (bf16[1,768]{1,0:T(2,128)(2,1)S(1)}, bf16[1,768]{1,0:T(2,128)(2,1)}, u32[]{:S(2)}) copy-start(bf16[1,768]{1,0:T(2,128)(2,1)} %get-tuple-element.46) | copy-start | bytes 4612
  136.0 22.7 %all-to-all-start.3 = ((bf16[16,24,384]{2,1,0:T(8,128)(2,1)}), bf16[16,24,384]{2,1,0:T(8,128)(2,1)S(1)}, u32[]{:S(2)}, u32[]{:S(2)}) async-start(bf16[16,24,384]{2,1,0:T(8,128)(2,1)} %get-tuple-element.33), calls=%async_computation.3 | async-start | bytes 589824 | tf_op jit(solution)/shard_map/all_to_all | solution.py:504
  140.6 6.6 %collective-permute-start.11 = (bf16[18,768]{1,0:T(8,128)(2,1)S(1)}, bf16[18,768]{1,0:T(8,128)(2,1)S(1)}, u32[]{:S(2)}, u32[]{:S(2)}) collective-permute-start(bf16[18,768]{1,0:T(8,128)(2,1)S(1)} %pad_maximum_fusion.5), channel_id=1, source_target_pairs={{1,0},{2,1},{3,2},{4,3},{5,4},{6,5},{7,6},{8,7},{9,8},{10,9},{11,1... | collective-permute-start | bytes 82952 | tf_op jit(solution)/shard_map/ppermute | solution.py:33
  145.3 12.7 %copy-start.26 = (f32[8,128]{1,0:T(8,128)S(1)}, f32[8,128]{1,0:T(8,128)}, u32[]{:S(2)}) copy-start(f32[8,128]{1,0:T(8,128)} %get-tuple-element.34) | copy-start | bytes 12292
  145.3 7.1 %collective-permute-start.10 = (bf16[18,768]{1,0:T(8,128)(2,1)S(1)}, bf16[18,768]{1,0:T(8,128)(2,1)S(1)}, u32[]{:S(2)}, u32[]{:S(2)}) collective-permute-start(bf16[18,768]{1,0:T(8,128)(2,1)S(1)} %pad_maximum_fusion.4), channel_id=1, source_target_pairs={{0,1},{1,2},{2,3},{3,4},{4,5},{5,6},{6,7},{7,8},{8,9},{9,10},{10,1... | collective-permute-start | bytes 82952 | tf_op jit(solution)/shard_map/ppermute | solution.py:32
  (16 other events, 73.8 us)
